TPU v7x, 32 devices: a whole 2x2x4 slice. The times are simulated.
32 devices in a mesh: dp: 8 (over z, y), head: 4 (over x, core).
Axes of the slice: x: 2, y: 2, z: 4, core: 2. Of those that a mesh axis runs over, the one named last changes fastest.
Arguments:
- tokens: float32 [64, 512, 768], P('dp', 'head'), may hold values from -6 to 6
- segment: int32 [64, 512], P('dp'), may hold values from 0 to 3, never falling along the last dimension, each value on 1 to 256 neighbouring positions
- modality: int32 [64, 512], P('dp', 'head'), may hold values from 0 to 1, as said below
- first_gain: float32 [2, 768], replicated, may hold values from 0.1 to 1.9
- first_shift: float32 [2, 768], replicated, may hold values from -1 to 1
- project_in: bfloat16 [768, 2304], replicated, may hold values from -0.21875 to 0.21875
- project_out: bfloat16 [768, 768], replicated, may hold values from -1.75 to 1.75
- second_gain: float32 [2, 768], replicated, may hold values from 0.1 to 1.9
- second_shift: float32 [2, 768], replicated, may hold values from -1 to 1
- up_weight: bfloat16 [2, 768, 3072], replicated, may hold values from -0.21875 to 0.21875
- down_weight: bfloat16 [2, 3072, 768], replicated, may hold values from -0.109375 to 0.109375
- cotangent: float32 [64, 512, 768], P('dp', 'head'), may hold values from -6 to 6
Outputs:
- output: float32 [64, 512, 768], P('dp', 'head')
- input_grad: float32 [64, 512, 768], P('dp', 'head')
- first_gain_grad: float32 [2, 768], P(None, 'dp')
- first_shift_grad: float32 [2, 768], P(None, 'dp')
- project_in_grad: float32 [768, 2304], P('dp')
- project_out_grad: float32 [768, 768], P('dp')
- second_gain_grad: float32 [2, 768], P(None, 'dp')
- second_shift_grad: float32 [2, 768], P(None, 'dp')
- up_weight_grad: float32 [2, 768, 3072], P(None, 'dp')
- down_weight_grad: float32 [2, 3072, 768], P(None, 'dp')
Inputs may be any that keep to these rules, and one draw needn't show every extreme that they name: Along each row segment numbers never fall; each segment is a run of 1 to 256 positions, and some run has exactly that many. On every device exactly 640 of its 1024 tokens have one modality and the others have the other one; which one is the larger varies by device.
All inputs are finite; a program needn't handle non-finite values.
Results may differ from a plain program's by a relative error of at most 0.015.
Values may be sent and summed in bfloat16 or wider, within the bound.
A program may use at most 320 MiB of HBM per device.

v0:
```python
import functools

import jax
import jax.numpy as jnp
from jax import lax
from jax.experimental import pallas as pl
from jax.experimental.pallas import tpu as pltpu
from jax.sharding import PartitionSpec as P

HEAD_DIM = 64
EXPERTS = 2
EPS = 1e-05
NEG = -1000000000.0
BLK = 128
CALLS = 2
VMEM_BYTES = 60 * 1024 * 1024
BF = jnp.bfloat16
F32 = jnp.float32
NT = (((1,), (1,)), ((), ()))
TN = (((0,), (0,)), ((), ()))


def mm(a, b):
    return jnp.dot(a, b, preferred_element_type=F32)


def mm_nt(a, b):
    return lax.dot_general(a, b, NT, preferred_element_type=F32)


def mm_tn(a, b):
    return lax.dot_general(a, b, TN, preferred_element_type=F32)


def bias_of(segc_ref, segr_ref, bias_ref):
    same = segc_ref[0] == segr_ref[0]
    bias_ref[...] = jnp.where(same, 0.0, NEG)


def attn_specs(sub, length, pairs):
    def part(i):
        return pl.BlockSpec((sub, 1, length, 128), lambda r, j, i=i: (0, r, 0, i * pairs + j))

    return part


def ffn_kernel(first, bits, info_ref, xm_ref, xo_ref, gm_ref, go_ref, u_ref, d_ref, *refs):
    if first:
        prev = (None,) * 4
        outs, grads = refs[:4], refs[4:8]
    else:
        prev, outs, grads = refs[:4], refs[4:8], refs[8:12]
    du_ref, dd_ref, act_ref, dh_ref = refs[-4:]
    e = pl.program_id(0)
    slots, model = xm_ref.shape
    cols = u_ref.shape[-1]
    tile = 256
    down = d_ref[0]

    @pl.when(e == 0)
    def _():
        for out in outs:
            out[slots - BLK :, :] = jnp.zeros((BLK, model), BF)

    du_ref[...] = jnp.zeros_like(du_ref)
    dd_ref[...] = jnp.zeros_like(dd_ref)

    def chunk(which, block, count):
        size = count * BLK
        rows = pl.ds(pl.multiple_of(block * BLK, BLK), size)
        x = (xm_ref, xo_ref)[which][rows, :]
        g = (gm_ref, go_ref)[which][rows, :]
        for n in range(cols // tile):
            part = slice(n * tile, (n + 1) * tile)
            h = mm(x, u_ref[0, :, part])
            da = mm_nt(g, down[part, :])
            cdf = 0.5 + 0.5 * lax.erf(h * 0.7071067811865476)
            pdf = 0.3989422804014327 * jnp.exp(-0.5 * h * h)
            act_ref[:size, part] = (h * cdf).astype(BF)
            dh_ref[:size, part] = (da * (cdf + h * pdf)).astype(BF)
        act = act_ref[:size, :]
        dh = dh_ref[:size, :]
        for slot, value in ((which, mm(act, down)), (2 + which, mm_nt(dh, u_ref[0]))):
            if prev[slot] is not None:
                value = value + prev[slot][rows, :].astype(F32)
            outs[slot][rows, :] = value.astype(BF)
        du_ref[...] += mm_tn(x, dh)
        dd_ref[...] += mm_tn(act, g)

    for which in range(2):
        n0 = info_ref[2 * which]
        n1 = info_ref[2 * which + 1]
        start = jnp.where(e == 0, 0, n0)
        count = jnp.where(e == 0, n0, n1)

        def four(i, carry, which=which, start=start):
            chunk(which, start + 4 * i, 4)
            return carry

        lax.fori_loop(0, count // 4, four, 0)
        at2 = start + (count // 4) * 4

        @pl.when((count // 2) % 2 == 1)
        def _(which=which, at2=at2):
            chunk(which, at2, 2)

        at1 = start + (count // 2) * 2

        @pl.when(count % 2 == 1)
        def _(which=which, at1=at1):
            chunk(which, at1, 1)

    up_keep, up_send, down_keep, down_send = grads
    groups = 1 << bits
    per = model // groups
    wide = down_keep.shape[2]
    xbit, ybit = info_ref[4], info_ref[5]
    for ref, here in ((up_keep, e == xbit), (up_send, e != xbit)):

        @pl.when(here)
        def _(ref=ref):
            for p in range(groups):
                ref[spot(p, range(bits))] = du_ref[p * per : (p + 1) * per, :].astype(BF)

    for y in range(2):
        for ref, here in ((down_keep, ybit == y), (down_send, ybit != y)):

            @pl.when(here)
            def _(ref=ref, y=y):
                for p in range(y, cols // wide, 2):
                    at = spot(p >> 1, range(bits - 3))
                    ref[at, e] = dd_ref[p * wide : (p + 1) * wide, :].astype(BF)


def spot(index, order):
    return functools.reduce(lambda acc, bit: 2 * acc + (index >> bit & 1), order, 0)


def ffn(call, info, x_mine, x_other, g_mine, g_other, up, down, partial, groups):
    slots, model = x_mine.shape
    hidden = up.shape[-1]
    cols = hidden // (2 * CALLS)
    bits = groups.bit_length() - 1
    whole = pl.BlockSpec((slots, model), lambda e, i: (0, 0), pipeline_mode=pl.Buffered(1))
    first = partial is None
    extra = () if first else tuple(partial)
    grads = [(groups, model // groups, model)] * 2
    grads += [(groups // 8, EXPERTS, hidden // groups, model)] * 2
    return pl.pallas_call(
        functools.partial(ffn_kernel, first, bits),
        grid_spec=pltpu.PrefetchScalarGridSpec(
            num_scalar_prefetch=1,
            grid=(EXPERTS,),
            in_specs=[whole] * 4
            + [
                pl.BlockSpec((1, model, cols), lambda e, i: (e, 0, i[6] * CALLS + call)),
                pl.BlockSpec((1, cols, model), lambda e, i: (e, i[6] * CALLS + call, 0)),
            ]
            + [whole] * len(extra),
            out_specs=[pl.BlockSpec((slots, model), lambda e, i: (0, 0))] * 4
            + [pl.BlockSpec(g, lambda e, i, n=len(g): (0,) * n) for g in grads],
            scratch_shapes=[
                pltpu.VMEM((model, cols), F32),
                pltpu.VMEM((cols, model), F32),
                pltpu.VMEM((4 * BLK, cols), BF),
                pltpu.VMEM((4 * BLK, cols), BF),
            ],
        ),
        out_shape=[jax.ShapeDtypeStruct((slots, model), BF)] * 4
        + [jax.ShapeDtypeStruct(g, BF) for g in grads],
        compiler_params=pltpu.CompilerParams(vmem_limit_bytes=VMEM_BYTES),
        cost_estimate=pl.CostEstimate(
            flops=12 * 2 * slots * model * cols, bytes_accessed=40 * 1024 * 1024,
            transcendentals=2 * 2 * slots * cols,
        ),
        name="ffn",
    )(info, x_mine, x_other, g_mine, g_other, up, down, *extra)


def peers():
    out = {}
    for axis in ("head", "dp"):
        me = lax.axis_index(axis)
        for b in range(lax.axis_size(axis).bit_length() - 1):
            bit = (me // (1 << b)) % 2
            out[axis, b] = bit, {axis: me + (1 - 2 * bit) * (1 << b)}
    return out


class Halving:
    def __init__(self, env, order, buf, gots, first, remote):
        self.rounds, path, prev = [], (), first
        for o, got in zip(order, gots):
            bit, partner = env[o]
            view = buf.at[path] if path else buf
            away, stay = view.at[1 - bit], view.at[bit]
            halves = (None, None) if prev is None else (prev.at[1 - bit], prev.at[bit])
            self.rounds.append((away, stay, *halves, remote(away, got, partner)))
            path, prev = path + (bit,), got
        self.result, self.last, self.at = buf.at[path], prev, 0
        self.done = False

    def send(self):
        away, stay, got_away, got_stay, copy = self.rounds[self.at]
        accumulate(away, got_away)
        copy.start()
        accumulate(stay, got_stay)

    def step(self):
        self.rounds[self.at][-1].wait_recv()
        self.at += 1
        if self.at < len(self.rounds):
            self.send()
        else:
            accumulate(self.result, self.last)
            self.done = True

    def close(self):
        for *_, copy in self.rounds:
            copy.wait_send()


def spots(ref):
    lead = len(ref.shape) - 2
    return [tuple(i >> b & 1 for b in range(lead)) for i in range(1 << lead)]


def accumulate(into, got):
    if got is not None:
        for at in spots(into):
            at = at or ...
            into[at] = into[at] + got[at]


def neighbours(env):
    me = lax.axis_index("head")
    out = [partner for _, partner in env.values()]
    for o in range(1, lax.axis_size("head")):
        if o & (o - 1):
            out.append({"head": (me // 4) * 4 + flipped(me % 4, o)})
    return out


def greet(env):
    barrier = pltpu.get_barrier_semaphore()
    partners = neighbours(env)
    for partner in partners:
        pl.semaphore_signal(barrier, inc=1, device_id=partner, device_id_type=pl.DeviceIdType.MESH)
    pl.semaphore_wait(barrier, len(partners))


class Copies:
    def __init__(self, send_sem, recv_sem, load_sem):
        self.send_sem, self.recv_sem, self.load_sem = send_sem, recv_sem, load_sem
        self.used, self.loads = 0, 0

    def remote(self, src, dst, to):
        s = self.used
        self.used += 1
        return pltpu.make_async_remote_copy(
            src_ref=src, dst_ref=dst, send_sem=self.send_sem.at[s], recv_sem=self.recv_sem.at[s],
            device_id=to, device_id_type=pl.DeviceIdType.MESH,
        )

    def local(self, src, dst):
        self.loads += 1
        return pltpu.make_async_copy(src, dst, self.load_sem.at[self.loads - 1])


def draw(refs, k):
    out = refs[:k]
    del refs[:k]
    return out


def others():
    me = lax.axis_index("head")
    return [(me // 4) * 4 + flipped(me % 4, o) for o in (3, 2, 1)]


def attn_fwd_kernel(
    segc_ref, segr_ref, q_ref, k_ref, v_ref, cot_ref, o_ref, lse_ref, got_ref,
    bias_ref, wide_ref, send_ref, *sems,
):
    sub, _, length, width = q_ref.shape
    seq = sub * length
    copies = Copies(*sems)
    me = lax.axis_index("head")
    targets = others()
    order = [*targets, me]
    loads = [copies.local(cot_ref.at[to], wide_ref.at[to]) for to in order]
    sends = [copies.remote(send_ref.at[to], got_ref.at[me], {"head": to}) for to in targets]
    stays = copies.local(send_ref.at[me], got_ref.at[me])
    barrier = pltpu.get_barrier_semaphore()
    at = pl.program_id(0) * pl.num_programs(1) + pl.program_id(1)

    @pl.when(at == 0)
    def _():
        for copy in loads:
            copy.start()
        for to in targets:
            pl.semaphore_signal(
                barrier, inc=1, device_id={"head": to}, device_id_type=pl.DeviceIdType.MESH
            )

    @pl.when(at == 1)
    def _():
        pl.semaphore_wait(barrier, len(targets))
        for to, load, copy in zip(order, loads, [*sends, stays]):
            load.wait()
            send_ref[to] = wide_ref[to].astype(BF)
            copy.start()

    @pl.when(at == pl.num_programs(0) * pl.num_programs(1) - 1)
    def _():
        for copy in [*sends, stays]:
            copy.wait()

    @pl.when(pl.program_id(1) == 0)
    def _():
        bias_of(segc_ref, segr_ref, bias_ref)

    q = q_ref[...].reshape(seq, width) * jnp.asarray(HEAD_DIM**-0.5, BF)
    k = k_ref[...].reshape(seq, width)
    vt = v_ref[...].reshape(seq, width).T
    lane = lax.broadcasted_iota(jnp.int32, (1, width), 1) // HEAD_DIM
    zero = jnp.zeros((), BF)
    per = width // HEAD_DIM
    step = 2 * length
    ks = [jnp.where(lane == h, k, zero) for h in range(per)]
    for b in range(seq // step):
        cols = slice(b * step, (b + 1) * step)
        parts = []
        for h in range(per):
            s = mm_nt(ks[h], q[cols]) + bias_ref[:, cols]
            top = jnp.max(s, axis=0, keepdims=True)
            e = jnp.exp(s - top)
            total = jnp.sum(e, axis=0, keepdims=True)
            parts.append(mm(vt[h * HEAD_DIM : (h + 1) * HEAD_DIM], e.astype(BF)) * (1.0 / total))
            lse_ref[0, 0, h : h + 1, cols] = top + jnp.log(total)
        out = jnp.concatenate(parts, axis=0).T.astype(BF)
        o_ref[2 * b : 2 * b + 2, 0] = out.reshape(2, length, width)


def attention_forward(segment, qkv, cotangent):
    sub, rows, length, wide = qkv.shape
    seq = sub * length
    model = wide // 3
    pairs = model // 128
    part = attn_specs(sub, length, pairs)
    hbm = pl.BlockSpec(memory_space=pl.ANY)
    return pl.pallas_call(
        attn_fwd_kernel,
        grid=(rows, pairs),
        in_specs=[
            pl.BlockSpec((1, seq, 1), lambda r, j: (r, 0, 0)),
            pl.BlockSpec((1, 1, seq), lambda r, j: (r, 0, 0)),
            part(0),
            part(1),
            part(2),
            hbm,
        ],
        out_specs=[part(0), pl.BlockSpec((1, 1, 2, seq), lambda r, j: (r, j, 0, 0)), hbm],
        out_shape=[
            jax.ShapeDtypeStruct((sub, rows, length, model), BF),
            jax.ShapeDtypeStruct((rows, pairs, 2, seq), F32),
            jax.ShapeDtypeStruct(cotangent.shape, BF),
        ],
        scratch_shapes=[
            pltpu.VMEM((seq, seq), F32),
            pltpu.VMEM(cotangent.shape, F32),
            pltpu.VMEM(cotangent.shape, BF),
            pltpu.SemaphoreType.DMA((3,)),
            pltpu.SemaphoreType.DMA((3,)),
            pltpu.SemaphoreType.DMA((5,)),
        ],
        compiler_params=pltpu.CompilerParams(
            collective_id=3, has_side_effects=True, vmem_limit_bytes=VMEM_BYTES
        ),
        cost_estimate=pl.CostEstimate(
            flops=8 * rows * seq * seq * model, bytes_accessed=8 * rows * seq * model,
            transcendentals=rows * seq * seq * model // HEAD_DIM,
        ),
        name="attn_fwd",
    )(segment[:, :, None], segment[:, None, :], qkv, qkv, qkv, cotangent)


def up_order(dp_bits):
    return [("dp", b) for b in range(dp_bits)]


def down_order(dp_bits):
    return [("dp", b) for b in range(1, dp_bits - 1)] + [("head", 1)]


def attention_orders(dp_bits):
    rest = [("dp", b) for b in range(1, dp_bits)]
    core, x, y = ("head", 0), ("head", 1), ("dp", 0)
    return [core, y, x] + rest, [core, x, y] + rest


def stream_scratch(order, tail, first):
    sizes = [len(order)] * (2 if first else 1) + [len(order) - r for r in range(1, len(order) + 1)]
    return [pltpu.VMEM((2,) * k + tail, BF) for k in sizes]


def attn_bwd_kernel(calls, dp_bits, *refs):
    refs = list(refs)
    segc_ref, segr_ref, q_ref, k_ref, v_ref, do_ref, lse_ref, low_ref, w_ref = draw(refs, 9)
    tok_ref, extra_ref, col_ref, gain_ref = draw(refs, 4)
    up_kept, up_came, down_kept, down_came = (draw(refs, calls) for _ in range(4))
    leaving_ref, in_ref, table_ref, tail_ref, up_ref, down_ref, back_ref, home_ref = draw(refs, 8)
    bias_ref, dqkv_ref, lowt_ref, acc_ref, first_ref, rows_ref = draw(refs, 6)
    env = peers()
    copies = Copies(*refs[-3:])
    r, j = pl.program_id(0), pl.program_id(1)
    rows, pairs = pl.num_programs(0), pl.num_programs(1)
    me = lax.axis_index("head")

    streams, loads = [], []
    order = up_order(dp_bits)[:2]
    for i in range(calls):
        buf, first, *gots = draw(refs, 2 + len(order))
        loads.append([copies.local(up_kept[i], buf), copies.local(up_came[i], first)])
        streams.append(Halving(env, order, buf, gots, first, copies.remote))
    order = down_order(dp_bits)
    buf, first, *gots = draw(refs, 2 + len(order))
    lead = dp_bits - 3
    loads.append([])
    for i in range(calls):
        for p in range(1 << lead):
            at = tuple(p >> (lead - 1 - b) & 1 for b in range(lead)) + (i,)
            loads[-1].append(copies.local(down_kept[i].at[p], buf.at[at]))
            loads[-1].append(copies.local(down_came[i].at[p], first.at[at]))
    streams.append(Halving(env, order, buf, gots, first, copies.remote))
    moves = []
    for o in range(1, 4):
        to = (me // 4) * 4 + flipped(me % 4, o)
        moves.append(copies.remote(leaving_ref.at[to], back_ref.at[me], {"head": to}))
    stays = [copies.local(leaving_ref.at[me], back_ref.at[me])]
    early = rows_ref.shape[1]
    homes = []
    for i in range(early):
        homes.append([copies.local(rows_ref.at[me, i], home_ref.at[me, i])])
        for to in others():
            homes[i].append(copies.remote(rows_ref.at[to, i], home_ref.at[me, i], {"head": to}))

    @pl.when((r == 0) & (j == 0))
    def _():
        for group in loads:
            for copy in group:
                copy.start()
        stays[0].start()
        greet(env)
        for stream, group in zip(reversed(streams), reversed(loads)):
            for copy in group:
                copy.wait()
            stream.send()
        for copy in moves:
            copy.start()

    @pl.when((r == rows - 1) & (j == 0))
    def _():
        streams[0].step()

    sub, _, length, width = q_ref.shape
    seq = sub * length
    model = dqkv_ref.shape[-1] // 3

    @pl.when(j == 0)
    def _():
        bias_of(segc_ref, segr_ref, bias_ref)

    scale = HEAD_DIM**-0.5
    q = q_ref[...].reshape(seq, width) * jnp.asarray(scale, BF)
    k = k_ref[...].reshape(seq, width)
    kt = k.T
    v = v_ref[...].reshape(seq, width)
    do = do_ref[...].reshape(seq, width)
    lane = lax.broadcasted_iota(jnp.int32, (1, width), 1) // HEAD_DIM
    zero = jnp.zeros((), BF)
    per = width // HEAD_DIM
    step = 2 * length
    dk = jnp.zeros((seq, width), F32)
    dv = jnp.zeros((seq, width), F32)
    dqs = [[] for _ in range(seq // step)]
    for h in range(per):
        kh = jnp.where(lane == h, k, zero)
        vh = jnp.where(lane == h, v, zero)
        qh = jnp.where(lane == h, q, zero)
        doh = jnp.where(lane == h, do, zero)
        for b in range(seq // step):
            cols = slice(b * step, (b + 1) * step)
            s = mm_nt(kh, q[cols]) + bias_ref[:, cols]
            p = jnp.exp(s - lse_ref[0, 0, h : h + 1, cols])
            dp = mm_nt(vh, do[cols])
            ds = (p * (dp - jnp.sum(p * dp, axis=0, keepdims=True))).astype(BF)
            dv = dv + mm(p.astype(BF), doh[cols])
            dk = dk + mm(ds, qh[cols])
            dqs[b].append(mm(kt[h * HEAD_DIM : (h + 1) * HEAD_DIM], ds) * scale)
    dq = jnp.concatenate([jnp.concatenate(d, axis=0).T for d in dqs], axis=0)
    for i, g in enumerate((dq, dk, dv)):
        at = pl.multiple_of(i * model + j * width, width)
        dqkv_ref[:, pl.ds(at, width)] = g.astype(BF)

    @pl.when((r == rows - 1) & (j == pairs - 1))
    def _():
        for stream in streams[1:]:
            stream.step()

    @pl.when(j == pairs - 1)
    def _():
        tile = 256
        lowt_ref[...] = low_ref[...].reshape(seq, model).T
        first_ref[...] = jnp.zeros_like(first_ref)

        @pl.when(r == 0)
        def _():
            acc_ref[...] = jnp.zeros_like(acc_ref)
            table_ref[...] = jnp.zeros_like(table_ref)

        def piece(n, carry):
            cols = pl.ds(pl.multiple_of(n * tile, tile), tile)
            part = dqkv_ref[:, cols]
            acc_ref[:, cols] += mm(lowt_ref[...], part)
            first_ref[...] += mm_nt(part, w_ref[:, cols])
            return carry

        lax.fori_loop(0, 3 * model // tile, piece, 0)
        for h in range(sub):
            grad = first_ref[h * length : (h + 1) * length, :]
            vision = col_ref[h, 0] > 0.5
            z, rstd = norm(tok_ref[h, 0].astype(F32))
            gain = jnp.where(vision, gain_ref[1:2], gain_ref[0:1])
            for i, term in enumerate((grad * z, grad)):
                for e, part in enumerate((jnp.where(vision, 0.0, term), jnp.where(vision, term, 0.0))):
                    at = 2 * i + e
                    table_ref[at : at + 1, :] += jnp.sum(part, axis=0, keepdims=True)
            tail = (extra_ref[h, 0] + norm_back(grad, gain, z, rstd)).astype(BF)

            @pl.when(r < early)
            def _(h=h, tail=tail):
                rows_ref[h, jnp.minimum(r, early - 1)] = tail

            @pl.when(r == early)
            def _(h=h, tail=tail):
                tail_ref[h, 0] = tail

        for i in range(early):

            @pl.when(r == i)
            def _(i=i):
                for copy in homes[i]:
                    copy.start()

    @pl.when((r == rows - 1) & (j == pairs - 1))
    def _():
        height = in_ref.shape[1]
        for p in range(in_ref.shape[0]):
            in_ref[p] = acc_ref[p * height : (p + 1) * height, :].astype(BF)
        while not all(stream.done for stream in streams):
            for stream in streams:
                if not stream.done:
                    stream.step()
        for i in range(calls):
            for at in spots(streams[i].result):
                up_ref[(i, *at)] = streams[i].result[at or ...]
        down_ref[...] = streams[-1].result[...]
        for copy in [*stays, *moves, *sum(homes, [])]:
            copy.wait()
        for stream in streams:
            stream.close()


def attention_backward(
    segment, qkv, grad, lse, low, weight, tok, extra, col, gain, up_kept, up_came, down_kept, down_came, leaving, dp_bits
):
    sub, rows, length, wide = qkv.shape
    seq = sub * length
    model = wide // 3
    pairs = model // 128
    groups = 1 << dp_bits
    calls = len(up_kept)
    part = attn_specs(sub, length, pairs)
    per, high = model // groups, down_kept[0].shape[2]
    row = pl.BlockSpec((sub, 1, length, model), lambda r, j: (0, r, 0, 0))
    hbm = pl.BlockSpec(memory_space=pl.ANY)

    def fixed(*shape):
        return pl.BlockSpec(shape, lambda r, j: (0,) * len(shape), pipeline_mode=pl.Buffered(1))

    up_kept, up_came = (
        [k.reshape((2,) * dp_bits + (per, model)) for k in ks] for ks in (up_kept, up_came)
    )
    ups, downs = up_order(dp_bits), down_order(dp_bits)
    scratch = [
        s
        for _ in range(calls)
        for s in [pltpu.VMEM((2,) * dp_bits + (per, model), BF)] * 2
        + [pltpu.VMEM((2,) * (dp_bits - 1 - i) + (per, model), BF) for i in range(2)]
    ]
    scratch += stream_scratch(downs, (high, model), True)
    sems = 2 * calls + len(downs) + 3 * rows
    loads = 2 * calls + 2 * calls * (groups // 8) + rows
    up_tail = (calls,) + (2,) * (dp_bits - 2) + (per, model)
    return pl.pallas_call(
        functools.partial(attn_bwd_kernel, calls, dp_bits),
        grid=(rows, pairs),
        in_specs=[
            pl.BlockSpec((1, seq, 1), lambda r, j: (r, 0, 0)),
            pl.BlockSpec((1, 1, seq), lambda r, j: (r, 0, 0)),
            part(0),
            part(1),
            part(2),
            part(0),
            pl.BlockSpec((1, 1, 2, seq), lambda r, j: (r, j, 0, 0)),
            row,
            fixed(*weight.shape),
            row,
            row,
            pl.BlockSpec((sub, 1, length, 1), lambda r, j: (0, r, 0, 0)),
            fixed(*gain.shape),
        ]
        + [hbm] * (4 * calls + 1),
        out_specs=[
            fixed(groups, per, wide), fixed(4, model), fixed(sub, 1, length, model),
            fixed(*up_tail), fixed(high, model), hbm, hbm,
        ],
        out_shape=[
            jax.ShapeDtypeStruct((groups, per, wide), BF),
            jax.ShapeDtypeStruct((4, model), F32),
            jax.ShapeDtypeStruct((sub, 1, length, model), BF),
            jax.ShapeDtypeStruct(up_tail, BF),
            jax.ShapeDtypeStruct((high, model), BF),
            jax.ShapeDtypeStruct(leaving.shape, BF),
            jax.ShapeDtypeStruct((sub, rows - 1, length, model), BF),
        ],
        scratch_shapes=[
            pltpu.VMEM((seq, seq), F32),
            pltpu.VMEM((seq, wide), BF),
            pltpu.VMEM((model, seq), BF),
            pltpu.VMEM((model, wide), F32),
            pltpu.VMEM((seq, model), F32),
            pltpu.VMEM((sub, rows - 1, length, model), BF),
        ]
        + scratch
        + [
            pltpu.SemaphoreType.DMA((sems,)),
            pltpu.SemaphoreType.DMA((sems,)),
            pltpu.SemaphoreType.DMA((loads,)),
        ],
        compiler_params=pltpu.CompilerParams(
            collective_id=1, has_side_effects=True, vmem_limit_bytes=VMEM_BYTES
        ),
        cost_estimate=pl.CostEstimate(
            flops=20 * rows * seq * seq * model + 4 * rows * seq * model * wide,
            bytes_accessed=100 * 1024 * 1024,
            transcendentals=rows * seq * seq * model // HEAD_DIM,
        ),
        name="attn_bwd",
    )(
        segment[:, :, None], segment[:, None, :], qkv, qkv, qkv, grad, lse, low, weight,
        tok, extra, col, gain,
        *up_kept, *up_came, *down_kept, *down_came, leaving,
    )


def finish_kernel(calls, dp_bits, *refs):
    refs = list(refs)
    up_ref, in_ref, out_ref = draw(refs, 3)
    tables = draw(refs, 3)
    last_ref, rows_ref, att_ref, up_out, down_ref, table_ref, home_ref = draw(refs, 7)
    env = peers()
    copies = Copies(*refs[-3:])
    remote = copies.remote
    core, x = env["head", 0][0], env["head", 1][0]
    me = lax.axis_index("head")
    groups = 1 << dp_bits
    model = home_ref.shape[-1]
    x_partner, core_partner = env["head", 1][1], env["head", 0][1]

    streams, loads = [], []
    for half, order in enumerate(attention_orders(dp_bits)):
        buf, *gots = draw(refs, 1 + len(order))
        loads.append([])
        lanes = buf.shape[-1]
        for i in range(4):
            ref, start = (out_ref, 0) if i == 3 else (in_ref, i * model)
            for p in range(groups):
                spot_of = {("head", 0): i >> 1, ("head", 1): i & 1}
                spot_of.update({("dp", b): p >> b & 1 for b in range(dp_bits)})
                cols = pl.ds(start + half * lanes, lanes)
                loads[-1].append(
                    copies.local(ref.at[p, :, cols], buf.at[tuple(spot_of[o] for o in order)])
                )
        streams.append(Halving(env, order, buf, gots, None, remote))
    order = up_order(dp_bits)[2:]
    for i in range(calls):
        buf, *gots = draw(refs, 1 + len(order))
        loads.append([copies.local(up_ref.at[i], buf)])
        streams.append(Halving(env, order, buf, gots, None, remote))
    (last_got,) = draw(refs, 1)
    sbuf, *sgots = draw(refs, 3 + dp_bits)

    for group in loads:
        for copy in group:
            copy.start()
    moves = []
    for o in range(1, 4):
        to = (me // 4) * 4 + flipped(me % 4, o)
        moves.append(remote(rows_ref.at[to], home_ref.at[me], {"head": to}))

    top, beyond = env["dp", dp_bits - 1]
    here, over = down_ref.at[x], down_ref.at[1 - x]
    last = remote(last_ref, last_got, beyond)
    to_x, to_core = remote(here, here, x_partner), remote(here, here, core_partner)
    forward = remote(over, over, core_partner)
    greet(env)

    @pl.when(top != core)
    def _():
        last.start()

    for stream, group in zip(streams, loads):
        for copy in group:
            copy.wait()
        stream.send()

    for at, ref in zip((0, 4, 6), tables):
        sbuf[at : at + ref.shape[0], :] = ref[...]
    sorder = [("head", 0), ("head", 1)] + [("dp", b) for b in range(dp_bits)]
    scopies = [remote(sbuf, got, env[o][1]) for o, got in zip(sorder, sgots)]
    scopies[0].start()
    home_ref[me] = rows_ref[me]

    gathers, after = [], []

    def spread(place, value):
        mine = place(x)
        mine[...] = value[...]
        for to, where in ((x_partner, after), (core_partner, gathers)):
            copy = remote(mine, mine, to)
            copy.start()
            where.append((copy, place))

    def att_place(half, side):
        at = (2 * core + side) * model + half * (model // 2)
        return att_ref.at[:, pl.ds(pl.multiple_of(at, 128), model // 2)]

    def up_place(call, side):
        at = (core * calls + call) * model
        return up_out.at[side, :, pl.ds(pl.multiple_of(at, 128), model)]

    rounds = max(len(sorder), max(len(stream.rounds) for stream in streams))
    for r in range(rounds):
        for i, stream in enumerate(streams):
            if not stream.done:
                stream.step()
                if stream.done:
                    if i < 2:
                        spread(functools.partial(att_place, i), stream.result)
                    else:
                        spread(functools.partial(up_place, i - 2), stream.result)
        if r < len(sorder):
            scopies[r].wait()
            sbuf[...] = sbuf[...] + sgots[r][...]
            if r + 1 < len(sorder):
                scopies[r + 1].start()
        if r == 1:
            for copy in moves:
                copy.start()

            @pl.when(top == core)
            def _():
                last.wait_recv()
                here[...] = last_ref[...] + last_got[...]
                to_x.start()
                to_core.start()

    table_ref[...] = sbuf[...]
    forwards = []
    for copy, place in after:
        copy.wait_recv()
        other = place(1 - x)
        forwards.append(remote(other, other, core_partner))
        forwards[-1].start()

    @pl.when(top == core)
    def _():
        to_x.wait_recv()
        forward.start()
        to_core.wait_send()
        to_x.wait_send()
        forward.wait_send()

    @pl.when(top != core)
    def _():
        last.wait_send()
        to_core.wait_recv()
        forward.wait_recv()

    for copy, _ in gathers:
        copy.wait()
    for copy in forwards:
        copy.wait()
    for copy, _ in after:
        copy.wait_send()
    for stream in streams:
        stream.close()
    for copy in moves:
        copy.wait()


def flipped(index, offset):
    low, high = index % 2, index // 2
    if offset & 1:
        low = 1 - low
    if offset & 2:
        high = 1 - high
    return 2 * high + low


def finish(dp_bits, up, down, in_term, out_term, tables, rows):
    assert rows.shape[0] == 4
    calls = up.shape[0]
    groups, per, model = out_term.shape
    high = down.shape[0]
    orders = attention_orders(dp_bits)
    ups = up_order(dp_bits)[2:]
    scratch = [s for o in orders for s in stream_scratch(o, (per, model // 2), False)]
    scratch += [s for _ in range(calls) for s in stream_scratch(ups, (per, model), False)]
    scratch.append(pltpu.VMEM((high, model), BF))
    scratch += [pltpu.VMEM((8, model), F32)] * (3 + dp_bits)
    sems = sum(map(len, orders)) + calls * len(ups) + 3 + 4 + 2 + dp_bits + 3 * (calls + 2)
    loads = 2 * 4 * groups + calls
    hbm = pl.BlockSpec(memory_space=pl.ANY)
    vmem = pl.BlockSpec(memory_space=pltpu.VMEM)
    return pl.pallas_call(
        functools.partial(finish_kernel, calls, dp_bits),
        in_specs=[hbm] * 3 + [vmem] * 5,
        out_specs=[vmem] * 5,
        out_shape=[
            jax.ShapeDtypeStruct((per, 4 * model), BF),
            jax.ShapeDtypeStruct((2, per, 2 * calls * model), BF),
            jax.ShapeDtypeStruct((2, high, model), BF),
            jax.ShapeDtypeStruct((8, model), F32),
            jax.ShapeDtypeStruct(rows.shape, BF),
        ],
        scratch_shapes=scratch
        + [
            pltpu.SemaphoreType.DMA((sems,)),
            pltpu.SemaphoreType.DMA((sems,)),
            pltpu.SemaphoreType.DMA((loads,)),
        ],
        compiler_params=pltpu.CompilerParams(
            collective_id=0, has_side_effects=True, vmem_limit_bytes=VMEM_BYTES
        ),
        cost_estimate=pl.CostEstimate(
            flops=0, bytes_accessed=100 * 1024 * 1024, transcendentals=0
        ),
        name="finish",
    )(up, in_term, out_term, *tables, down, rows)


def enter_kernel(tokens_ref, modality_ref, gain_ref, shift_ref, w_ref, *refs):
    refs = list(refs)
    tok_ref, kind_ref, col_ref, low_ref, qkv_ref, wide_ref, send_ref = draw(refs, 7)
    copies = Copies(*refs)
    me = lax.axis_index("head")
    heads, rows, length, model = tok_ref.shape
    core = me % 2
    targets = others()
    loads = {
        (o, r): copies.local(tokens_ref.at[to, r], wide_ref.at[to, r])
        for r in range(rows)
        for o, to in enumerate([*targets, me])
    }
    kinds = [copies.remote(modality_ref.at[to // 2], kind_ref.at[me], {"head": to}) for to in targets]
    sends = {
        (o, r): copies.remote(send_ref.at[to, r], tok_ref.at[me, r], {"head": to})
        for r in range(rows)
        for o, to in enumerate(targets)
    }
    for copy in loads.values():
        copy.start()
    barrier = pltpu.get_barrier_semaphore()
    for to in targets:
        pl.semaphore_signal(
            barrier, inc=1, device_id={"head": to}, device_id_type=pl.DeviceIdType.MESH
        )
    pl.semaphore_wait(barrier, len(targets))
    for copy in kinds:
        copy.start()
    kind_ref[me] = modality_ref[me // 2]
    for r in range(rows):
        for o, to in enumerate(targets):
            loads[o, r].wait()
            send_ref[to, r] = wide_ref[to, r].astype(BF)
            sends[o, r].start()
        loads[len(targets), r].wait()
        tok_ref[me, r] = wide_ref[me, r].astype(BF)
    for copy in kinds:
        copy.wait()
    ones = jnp.ones((8, length), BF)
    row = lax.broadcasted_iota(jnp.int32, (8, length), 0)
    for r in range(rows):
        for o in range(len(targets)):
            sends[o, r].wait_recv()
        for h in range(heads):
            kind = kind_ref[h, core, r : r + 1, :].astype(F32)
            kind = jnp.where(row == 0, jnp.broadcast_to(kind, (8, length)), 0.0).astype(BF)
            kind = mm_tn(kind, ones)[:, :1]
            col_ref[h, r] = kind
            z, _ = norm(tok_ref[h, r].astype(F32))
            low = z * jnp.where(kind < 0.5, gain_ref[0:1], gain_ref[1:2])
            low_ref[h, r] = (low + jnp.where(kind < 0.5, shift_ref[0:1], shift_ref[1:2])).astype(BF)
        low = low_ref[:, r].reshape(heads * length, model)
        for n in range(w_ref.shape[1] // model):
            cols = slice(n * model, (n + 1) * model)
            part = mm(low, w_ref[:, cols]).astype(BF)
            qkv_ref[:, r, :, cols] = part.reshape(heads, length, model)
    for copy in sends.values():
        copy.wait_send()


def enter(tokens, modality, gain, shift, weight):
    heads, rows, _, model = tokens.shape
    assert heads == 4
    vmem = pl.BlockSpec(memory_space=pltpu.VMEM)
    sems = 3 * rows + 3
    return pl.pallas_call(
        enter_kernel,
        in_specs=[pl.BlockSpec(memory_space=pl.ANY)] + [vmem] * 4,
        out_specs=[vmem] * 5,
        out_shape=[
            jax.ShapeDtypeStruct(tokens.shape, BF),
            jax.ShapeDtypeStruct((heads,) + modality.shape[1:], jnp.int32),
            jax.ShapeDtypeStruct(tokens.shape[:3] + (1,), F32),
            jax.ShapeDtypeStruct(tokens.shape, BF),
            jax.ShapeDtypeStruct(tokens.shape[:3] + weight.shape[1:], BF),
        ],
        scratch_shapes=[
            pltpu.VMEM(tokens.shape, F32),
            pltpu.VMEM(tokens.shape, BF),
            pltpu.SemaphoreType.DMA((sems,)),
            pltpu.SemaphoreType.DMA((sems,)),
            pltpu.SemaphoreType.DMA((4 * rows,)),
        ],
        compiler_params=pltpu.CompilerParams(
            collective_id=2, has_side_effects=True, vmem_limit_bytes=VMEM_BYTES
        ),
        cost_estimate=pl.CostEstimate(
            flops=2 * tokens.size * weight.shape[1], bytes_accessed=40 * 1024 * 1024,
            transcendentals=0,
        ),
        name="enter",
    )(tokens, modality, gain, shift, weight)


def norm(values):
    mean = jnp.mean(values, axis=-1, keepdims=True)
    centered = values - mean
    rstd = lax.rsqrt(jnp.mean(centered * centered, axis=-1, keepdims=True) + EPS)
    return centered * rstd, rstd


def pick(table, kind):
    return jnp.where(kind == 0, table[0], table[1])


def norm_back(grad, gains, z, rstd):
    q = grad * gains
    return rstd * (
        q
        - jnp.mean(q, axis=-1, keepdims=True)
        - z * jnp.mean(q * z, axis=-1, keepdims=True)
    )


def by_expert(values, kind):
    first = jnp.sum(jnp.where(kind == 0, values, 0.0), axis=0)
    second = jnp.sum(jnp.where(kind == 0, 0.0, values), axis=0)
    return jnp.stack([first, second])


def flip(axis, size, bit):
    return functools.partial(
        lax.ppermute, axis_name=axis, perm=[(i, i ^ (1 << bit)) for i in range(size)]
    )


def take(values, dim, index):
    return lax.dynamic_index_in_dim(values, index, dim, keepdims=False)


def body(sizes, tokens, segment, modality, first_gain, first_shift, project_in, project_out,
         second_gain, second_shift, up_weight, down_weight, cotangent):
    heads, groups = sizes["head"], sizes["dp"]
    row_count, length, model = tokens.shape
    rows = row_count // heads
    count = row_count * length
    hidden = up_weight.shape[-1]
    me_h, me_d = lax.axis_index("head"), lax.axis_index("dp")
    core = me_h % 2
    head_bits = heads.bit_length() - 1
    dp_bits = groups.bit_length() - 1
    assert heads == 1 << head_bits and groups == 1 << dp_bits and head_bits >= 2
    hflip = [flip("head", heads, b) for b in range(head_bits)]
    dflip = [flip("dp", groups, b) for b in range(dp_bits)]

    grid = (heads, rows, length)
    tok, kinds, col, low1, qkv = enter(
        tokens.reshape(*grid, model), modality.reshape(heads // 2, 2, rows, length),
        first_gain, first_shift, project_in,
    )
    seg = lax.dynamic_slice_in_dim(segment, me_h * rows, rows, 0)
    kind = take(kinds, 1, core).reshape(count)
    kcol = col.reshape(count, 1)

    flat = tok.astype(F32).reshape(count, model)
    context, lse, cot = attention_forward(seg, qkv, cotangent.reshape(*grid, model))
    cot = cot.reshape(count, model)
    ctx = context.reshape(count, model)
    attention = mm(ctx, project_out)
    residual = flat + attention
    z2, rstd2 = norm(residual)
    gain2 = pick(second_gain, kcol)
    low2 = (z2 * gain2 + pick(second_shift, kcol)).astype(BF)

    slots = count + BLK
    is0 = (kind == 0).astype(F32).reshape(count // BLK, BLK)
    tri = jnp.triu(jnp.ones((BLK, BLK), F32))
    inner = mm(is0, tri)
    ends = jnp.cumsum(inner[:, -1])
    before = (inner + (ends - inner[:, -1])[:, None]).reshape(count).astype(jnp.int32)
    n0 = ends[-1].astype(jnp.int32)
    blocks0 = (n0 + BLK - 1) // BLK
    blocks1 = (count - n0 + BLK - 1) // BLK
    rank1 = jnp.arange(count, dtype=jnp.int32) - before
    slot = jnp.where(kind == 0, before - 1, blocks0 * BLK + rank1)
    place = (slot[None, :] == jnp.arange(slots, dtype=jnp.int32)[:, None]).astype(BF)

    near = hflip[0]
    g_mine = mm(place, cot).astype(BF)
    g_other = near(g_mine)
    zeros = jnp.sum(kinds == 0, axis=(0, 2, 3))
    full = jnp.stack([(zeros + BLK - 1) // BLK, (count - zeros + BLK - 1) // BLK], axis=1)
    blocks, blocks_other = take(full, 0, core), take(full, 0, 1 - core)
    xbit = (me_h // 2) % 2
    ybit = me_d % 2
    info = jnp.concatenate([blocks, blocks_other, jnp.stack([xbit, ybit, core])]).astype(jnp.int32)
    x_mine = mm(place, low2).astype(BF)
    x_other = near(x_mine)

    partial, kept, came = None, ([], []), ([], [])
    for call in range(CALLS):
        *partial, up_keep, up_send, down_keep, down_send = ffn(
            call, info, x_mine, x_other, g_mine, g_other, up_weight, down_weight, partial, groups
        )
        kept[0].append(up_keep)
        kept[1].append(down_keep)
        came[0].append(hflip[1](up_send))
        came[1].append(dflip[0](down_send))

    partial, early = lax.optimization_barrier((partial, [c[:-1] for c in came]))
    came = [e + c[-1:] for e, c in zip(early, came)]
    branch_mine, branch_other, dx_mine, dx_other = partial
    dx = dx_mine + near(dx_other)
    second_grad = mm_tn(place, dx)
    branch = mm_tn(place, branch_mine + near(branch_other))
    leaving = (attention + branch).astype(BF).reshape(*grid, model)

    cot32 = cot.astype(F32)
    gain2_term = by_expert(second_grad * z2, kcol)
    shift2_term = by_expert(second_grad, kcol)
    extra = norm_back(second_grad, gain2, z2, rstd2)
    attention_low = (cot32 + extra).astype(BF)
    out_term = mm_tn(ctx, attention_low)
    context_grad = mm_nt(attention_low, project_out).astype(BF)
    in_term, table1, tail, up_sum, down_sum, back, home0 = attention_backward(
        seg, qkv, context_grad.reshape(context.shape), lse, low1, project_in,
        tok, extra.reshape(*grid, model), col, first_gain,
        kept[0], came[0], kept[1], came[1], leaving, dp_bits,
    )
    output = tokens + back.reshape(row_count, length, model).astype(F32)
    att_sum, up_sum, down_sum, table, home = finish(
        dp_bits, up_sum, down_sum, in_term,
        out_term.astype(BF).reshape(groups, model // groups, model),
        (table1, gain2_term, shift2_term), tail,
    )
    home = jnp.concatenate([home0, home], axis=1)
    input_grad = cotangent + home.reshape(row_count, length, model).astype(F32)

    up_grad, down_grad = up_sum.astype(F32), down_sum.astype(F32)
    in_grad = att_sum[:, : 3 * model].astype(F32)
    out_grad = att_sum[:, 3 * model :].astype(F32)
    tables = lax.dynamic_slice_in_dim(table, me_d * (model // groups), model // groups, 1)
    tables = tables.reshape(4, EXPERTS, model // groups)
    return (
        output, input_grad, tables[0], tables[1], in_grad, out_grad, tables[2], tables[3],
        up_grad, down_grad,
    )


def solution(mesh):
    return jax.shard_map(
        functools.partial(body, dict(mesh.shape)),
        mesh=mesh,
        in_specs=(
            P("dp", "head", None),
            P("dp", None),
            P("dp", "head"),
            P(),
            P(),
            P(),
            P(),
            P(),
            P(),
            P(),
            P(),
            P("dp", "head", None),
        ),
        out_specs=(
            P("dp", "head", None),
            P("dp", "head", None),
            P(None, "dp"),
            P(None, "dp"),
            P("dp", None),
            P("dp", None),
            P(None, "dp"),
            P(None, "dp"),
            P(None, "dp", None),
            P(None, "dp", None),
        ),
        check_vma=False,
    )
```

profile of v0, /device:TPU:0, one launch (start us, length us, event | category | flops | bytes accessed | tf_op | source)
XLA Modules:
  0.0 318.1 jit_solution(6529010119600148241)
XLA Ops:
  0.7 0.8 fusion.48
  1.5 0.7 constant_dynamic-slice_fusion.3
  2.2 29.9 %enter.1 = (bf16[4,2,128,768]{3,2,1,0:T(8,128)(2,1)}, s32[4,2,2,128]{3,2,1,0:T(2,128)}, f32[4,2,128,1]{3,2,1,0:T(8,128)}, bf16[4,2,128,768]{3,2,1,0:T(8,128)(2,1)}, bf16[4,2,128,2304]{3,2,1,0:T(8,128)(2,1)}) custom-call(f32[4,2,128,768]{3,2,1,0:T(8,128)} %bitcast.64, s32[2,2,2,128]{3,2,1,0:T(2,128)} %bitcast.71, f32[2,768]{1,0:T(2,128)} %refs_12_.1, ...), custom_call_target="tpu_custom_call" | custom-call | flops 3623878656 | bytes 41943040 | tf_op jit(solution)/shard_map/enter/pallas_call | solution.py:931
  32.2 0.7 dynamic-slice_compare_fusion
  32.9 0.2 fusion.26
  33.2 0.5 slice.43
  34.4 0.2 subtract_reduce_fusion
  34.6 0.6 broadcast_in_dim.74.segr_ref.refs_1_
  35.2 1.0 copy.23.segc_ref.refs_0_
  36.3 26.5 %attn_fwd.1 = (bf16[4,2,128,768]{3,2,1,0:T(8,128)(2,1)}, f32[2,6,2,512]{3,2,1,0:T(2,128)}, bf16[4,2,128,768]{3,2,1,0:T(8,128)(2,1)}) custom-call(s32[2,512,1]{2,1,0:T(8,128)} %copy.23.segc_ref.refs_0_, s32[2,1,512]{2,1,0:T(1,128)} %broadcast_in_dim.74.segr_ref.refs_1_, bf16[4,2,128,2304]{3,2,1,0:T(8,128)(2,1)} %get-tuple-element.52.q_ref.k_ref.v_ref.refs_2_.refs_3_.refs_4_, ...), custom_call_target="tpu_custom_call" | custom-call | flops 3221225472 | bytes 6291456 | tf_op jit(solution)/shard_map/attn_fwd/pallas_call | solution.py:352
  62.8 4.9 %fusion.5.gm_ref = bf16[1152,768]{1,0:T(8,128)(2,1)} fusion(bf16[1024,768]{1,0:T(8,128)(2,1)} %bitcast.68, s32[1024]{0:T(1024)S(1)} %fusion.32), kind=kOutput, calls=%fused_computation.8 | convolution fusion | flops 1814003712 | bytes 3346432 | tf_op jit(solution)/shard_map/dot_general | solution.py:24
  67.8 0.2 compare_reduce_fusion
  68.0 4.5 %fusion.38 = (f32[1024]{0:T(1024)S(1)}, f32[1024,768]{1,0:T(8,128)S(1)}, f32[1024,768]{1,0:T(8,128)}) fusion(bf16[4,2,128,768]{3,2,1,0:T(8,128)(2,1)S(1)} %copy-done.5, bf16[1024,768]{1,0:T(8,128)(2,1)} %bitcast.66, bf16[768,768]{1,0:T(8,128)(2,1)S(1)} %copy-done), kind=kOutput, calls=%fused_computation.89 | convolution fusion | flops 1210317824 | bytes 10620928 | tf_op jit(solution)/shard_map/dot_general | solution.py:24
  72.5 0.5 multiply_reduce_fusion.1
  73.0 0.2 copy-done.15
  73.3 4.0 %fusion.4.xm_ref = bf16[1152,768]{1,0:T(8,128)(2,1)} fusion(s32[1024]{0:T(1024)S(1)} %fusion.32, f32[1024,768]{1,0:T(8,128)S(1)} %get-tuple-element.113, f32[768]{0:T(1024)S(1)} %get-tuple-element.107, f32[768]{0:T(1024)S(1)} %get-tuple-element.106, f32[768]{0:T(1024)S(1)} %get-tuple-element.122, f32[768]{0:T(1024)S(1)} %get-tuple-element.123, ...), kind=kOutput, calls=%fused_computation.7 | convolution fusion | flops 1819508736 | bytes 4940800 | tf_op jit(solution)/shard_map/dot_general | solution.py:24
  77.3 0.5 collective-permute-start
  78.0 0.2 fusion.35
  78.2 0.6 concatenate.6.info_ref
  78.8 2.7 collective-permute-done.xo_ref
  81.5 30.5 %ffn.2 = (bf16[1152,768]{1,0:T(8,128)(2,1)}, bf16[1152,768]{1,0:T(8,128)(2,1)}, bf16[1152,768]{1,0:T(8,128)(2,1)}, bf16[1152,768]{1,0:T(8,128)(2,1)}, bf16[8,96,...) custom-call(s32[7]{0:T(128)} %concatenate.6.info_ref, ...), custom_call_target="tpu_custom_call" | custom-call | flops 16307453952 | bytes 41943040 | tf_op jit(solution)/shard_map/ffn/pallas_call | solution.py:149
  111.9 1.4 collective-permute-start.2
  113.3 1.5 collective-permute-start.3
  114.9 32.6 %ffn.3 = (bf16[1152,768]{1,0:T(8,128)(2,1)}, bf16[1152,768]{1,0:T(8,128)(2,1)}, bf16[1152,768]{1,0:T(8,128)(2,1)}, bf16[1152,768]{1,0:T(8,128)(2,1)}, bf16[8,96,...) custom-call(s32[7]{0:T(128)} %concatenate.6.info_ref, ...), custom_call_target="tpu_custom_call" | custom-call | flops 16307453952 | bytes 41943040 | tf_op jit(solution)/shard_map/ffn/pallas_call | solution.py:149
  147.5 1.0 copy-done.17
  148.5 0.7 collective-permute-start.5
  149.2 0.4 collective-permute-start.6
  149.7 2.8 collective-permute-done.4
  152.4 6.6 %select_reduce_fusion.1 = (f32[768]{0:T(1024)S(1)}, f32[768]{0:T(1024)S(1)}, f32[1024]{0:T(1024)S(1)}, f32[1024]{0:T(1024)S(1)}, f32[768]{0:T(1024)S(1)}, /*index=5*/f32[768]{0:T(1024)S(1)}, f32[1024,768]{1,0:T(8,128)S(1)}) fusion(pred[1024]{0:T(1024)(128)(4,1)S(1)} %eq.63, f32[768]{0:T(1024)S(1)} %get-tuple-element.122, f32[768]{0:T(1024)S(1)} %get-tuple-element.123, ...), kind=kOutput, calls=%fused_computation.15 | convolution fusion | flops 1826581504 | bytes 9870336 | tf_op jit(solution)/shard_map/dot_general | solution.py:32
  159.1 3.0 add_convert_fusion.1
  162.1 2.6 convolution_convert_fusion
  164.6 0.6 pad_maximum_fusion.2.refs_5_
  165.2 0.6 pad_maximum_fusion.1.refs_4_
  165.8 2.6 convolution_convert_fusion.1
  168.4 3.7 %add_convert_fusion = bf16[1024,768]{1,0:T(8,128)(2,1)} fusion(f32[1024,768]{1,0:T(8,128)S(1)} %copy-done.4, bf16[1152,768]{1,0:T(8,128)(2,1)S(1)} %copy-done.18, bf16[1152,768]{1,0:T(8,128)(2,1)S(1)} %collective-permute-done.7, s32[1024]{0:T(1024)S(1)} %fusion.32), kind=kOutput, calls=%fused_computation.18 | convolution fusion | flops 1815576576 | bytes 8261632 | tf_op jit(solution)/shard_map/dot_general | solution.py:32
  172.1 5.1 %collective-permute-done.5 = bf16[8,96,768]{2,1,0:T(8,128)(2,1)} collective-permute-done((bf16[8,96,768]{2,1,0:T(8,128)(2,1)}, bf16[8,96,768]{2,1,0:T(8,128)(2,1)}, u32[]{:S(2)}, u32[]{:S(2)}) %collective-permute-start.5) | collective-permute-done | bytes 1179680 | tf_op jit(solution)/shard_map/ppermute | solution.py:1062
  177.2 0.4 collective-permute-done.6.refs_20_
  177.6 65.0 %attn_bwd.1 = (bf16[8,96,2304]{2,1,0:T(8,128)(2,1)}, f32[4,768]{1,0:T(4,128)}, bf16[4,1,128,768]{3,2,1,0:T(8,128)(2,1)}, bf16[2,2,96,768]{3,2,1,0:T(8,128)(2,1)}...) custom-call(s32[2,512,1]{2,1,0:T(8,128)} %copy.23.segc_ref.refs_0_, ...), custom_call_target="tpu_custom_call" | custom-call | flops 15300820992 | bytes 104857600 | tf_op jit(solution)/shard_map/attn_bwd/pallas_call | solution.py:606
  242.7 59.8 %finish.1 = (bf16[96,3072]{1,0:T(8,128)(2,1)}, bf16[2,96,3072]{2,1,0:T(8,128)(2,1)}, bf16[2,384,768]{2,1,0:T(8,128)(2,1)}, f32[8,768]{1,0:T(8,128)}, bf16[4,1,128,768]{3,2,1,0:T(8,128)(2,1)}) custom-call(bf16[2,2,96,768]{3,2,1,0:T(8,128)(2,1)} %get-tuple-element.84.refs_0_, bf16[8,96,2304]{2,1,0:T(8,128)(2,1)} %get-tuple-element.85.refs_1_, ...), custom_call_target="tpu_custom_call" | custom-call | bytes 104857600 | tf_op jit(solution)/shard_map/finish/pallas_call | solution.py:838
  302.5 1.8 slice_convert_fusion.1
  304.3 2.0 slice_convert_fusion
  306.3 4.0 %convert_add_fusion.1 = f32[8,128,768]{2,1,0:T(8,128)} fusion(f32[8,128,768]{2,1,0:T(8,128)} %param.12, bf16[4,2,128,768]{3,2,1,0:T(8,128)(2,1)S(1)} %copy-done.8), kind=kLoop, calls=%fused_computation.12 | loop fusion | flops 1572864 | bytes 7864320 | tf_op jit(solution)/shard_map/add | solution.py:1085
  310.3 0.9 constant_dynamic-slice_fusion
  311.2 0.6 fusion.39
  311.9 0.3 copy-done.3
  312.2 2.2 convert_add_fusion
  314.4 1.7 convert_element_type.86
  316.1 1.6 convert_element_type.87
  (62 shorter events, 0.7 us)
Async XLA Ops:
  0.6 67.4 %copy-start = (bf16[768,768]{1,0:T(8,128)(2,1)S(1)}, bf16[768,768]{1,0:T(8,128)(2,1)}, u32[]{:S(2)}) copy-start(bf16[768,768]{1,0:T(8,128)(2,1)} %param.18) | copy-start | bytes 3538948
  62.8 5.0 %copy-start.13 = (f32[4,2,128,1]{3,2,1,0:T(8,128)S(1)}, f32[4,2,128,1]{3,2,1,0:T(8,128)}, u32[]{:S(2)}) copy-start(f32[4,2,128,1]{3,2,1,0:T(8,128)} %get-tuple-element.57.refs_11_) | copy-start | bytes 12292
  62.8 5.2 %copy-start.5 = (bf16[4,2,128,768]{3,2,1,0:T(8,128)(2,1)S(1)}, bf16[4,2,128,768]{3,2,1,0:T(8,128)(2,1)}, u32[]{:S(2)}) copy-start(bf16[4,2,128,768]{3,2,1,0:T(8,128)(2,1)} %get-tuple-element.54.refs_9_) | copy-start | bytes 4718596
  67.8 11.1 %collective-permute-start.1 = (bf16[1152,768]{1,0:T(8,128)(2,1)}, bf16[1152,768]{1,0:T(8,128)(2,1)}, u32[]{:S(2)}, u32[]{:S(2)}) collective-permute-start(bf16[1152,768]{1,0:T(8,128)(2,1)} %fusion.5.gm_ref), channel_id=1, source_target_pairs={{0,1},{1,0},{2,3},{3,2},{4,5},{5,4},{6,7},{7,6},{8,9},{9,8},{10,11... | collective-permute-start | bytes 5308424 | tf_op jit(solution)/shard_map/ppermute | solution.py:1045
  72.5 4.8 %copy-start.1 = (f32[1024,768]{1,0:T(8,128)}, f32[1024,768]{1,0:T(8,128)S(1)}, u32[]{:S(2)}) copy-start(f32[1024,768]{1,0:T(8,128)S(1)} %get-tuple-element.113) | copy-start | bytes 9437188
  72.5 0.7 copy-start.15
  72.5 0.8 copy-start.16
  73.3 4.5 %copy-start.14 = (s32[4,2,2,128]{3,2,1,0:T(2,128)S(1)}, s32[4,2,2,128]{3,2,1,0:T(2,128)}, u32[]{:S(2)}) copy-start(s32[4,2,2,128]{3,2,1,0:T(2,128)} %get-tuple-element.56) | copy-start | bytes 24580
  77.3 4.2 %collective-permute-start = (bf16[1152,768]{1,0:T(8,128)(2,1)}, bf16[1152,768]{1,0:T(8,128)(2,1)}, u32[]{:S(2)}, u32[]{:S(2)}) collective-permute-start(bf16[1152,768]{1,0:T(8,128)(2,1)} %fusion.4.xm_ref), channel_id=1, source_target_pairs={{0,1},{1,0},{2,3},{3,2},{4,5},{5,4},{6,7},{7,6},{8,9},{9,8},{10,11... | collective-permute-start | bytes 5308424 | tf_op jit(solution)/shard_map/ppermute | solution.py:1053
  111.9 35.5 %collective-permute-start.2 = (bf16[8,96,768]{2,1,0:T(8,128)(2,1)}, bf16[8,96,768]{2,1,0:T(8,128)(2,1)S(1)}, u32[]{:S(2)}, u32[]{:S(2)}) collective-permute-start(bf16[8,96,768]{2,1,0:T(8,128)(2,1)} %get-tuple-element.66), channel_id=1, source_target_pairs={{0,2},{1,3},{2,0},{3,1},{4,6},{5,7},{6,4},{7,5},{8,10},{9,11},{10,... | collective-permute-start | bytes 3538952 | tf_op jit(solution)/shard_map/ppermute | solution.py:1062
  113.3 34.1 %collective-permute-start.3 = (bf16[1,2,384,768]{3,2,1,0:T(8,128)(2,1)}, bf16[1,2,384,768]{3,2,1,0:T(8,128)(2,1)}, u32[]{:S(2)}, u32[]{:S(2)}) collective-permute-start(bf16[1,2,384,768]{3,2,1,0:T(8,128)(2,1)} %get-tuple-element.67), channel_id=1, source_target_pairs={{0,4},{4,0},{8,12},{12,8},{16,20},{20,16},{24,28},{28,24},{1,5},{5... | collective-permute-start | bytes 3538952 | tf_op jit(solution)/shard_map/ppermute | solution.py:1063
  147.5 1.1 copy-start.17
  148.5 3.9 %collective-permute-start.4 = (bf16[1152,768]{1,0:T(8,128)(2,1)}, bf16[1152,768]{1,0:T(8,128)(2,1)S(1)}, u32[]{:S(2)}, u32[]{:S(2)}) collective-permute-start(bf16[1152,768]{1,0:T(8,128)(2,1)} %get-tuple-element.69), channel_id=1, source_target_pairs={{0,1},{1,0},{2,3},{3,2},{4,5},{5,4},{6,7},{7,6},{8,9},{9,8},{10,11... | collective-permute-start | bytes 5308424 | tf_op jit(solution)/shard_map/ppermute | solution.py:1068
  148.5 28.7 %collective-permute-start.5 = (bf16[8,96,768]{2,1,0:T(8,128)(2,1)}, bf16[8,96,768]{2,1,0:T(8,128)(2,1)}, u32[]{:S(2)}, u32[]{:S(2)}) collective-permute-start(bf16[8,96,768]{2,1,0:T(8,128)(2,1)} %get-tuple-element.75), channel_id=1, source_target_pairs={{0,2},{1,3},{2,0},{3,1},{4,6},{5,7},{6,4},{7,5},{8,10},{9,11},{10,... | collective-permute-start | bytes 3538952 | tf_op jit(solution)/shard_map/ppermute | solution.py:1062
  149.2 9.8 %copy-start.7 = (bf16[4,2,128,768]{3,2,1,0:T(8,128)(2,1)S(1)}, bf16[4,2,128,768]{3,2,1,0:T(8,128)(2,1)}, u32[]{:S(2)}) copy-start(bf16[4,2,128,768]{3,2,1,0:T(8,128)(2,1)} %get-tuple-element.53) | copy-start | bytes 4718596
  149.2 28.4 %collective-permute-start.6 = (bf16[1,2,384,768]{3,2,1,0:T(8,128)(2,1)}, bf16[1,2,384,768]{3,2,1,0:T(8,128)(2,1)}, u32[]{:S(2)}, u32[]{:S(2)}) collective-permute-start(bf16[1,2,384,768]{3,2,1,0:T(8,128)(2,1)} %get-tuple-element.79), channel_id=1, source_target_pairs={{0,4},{4,0},{8,12},{12,8},{16,20},{20,16},{24,28},{28,24},{1,5},{5... | collective-permute-start | bytes 3538952 | tf_op jit(solution)/shard_map/ppermute | solution.py:1063
  149.7 18.7 %collective-permute-start.7 = (bf16[1152,768]{1,0:T(8,128)(2,1)}, bf16[1152,768]{1,0:T(8,128)(2,1)S(1)}, u32[]{:S(2)}, u32[]{:S(2)}) collective-permute-start(bf16[1152,768]{1,0:T(8,128)(2,1)} %get-tuple-element.81), channel_id=1, source_target_pairs={{0,1},{1,0},{2,3},{3,2},{4,5},{5,4},{6,7},{7,6},{8,9},{9,8},{10,11... | collective-permute-start | bytes 5308424 | tf_op jit(solution)/shard_map/ppermute | solution.py:1070
  152.4 6.6 %copy-start.2 = (f32[1024,768]{1,0:T(8,128)S(1)}, f32[1024,768]{1,0:T(8,128)}, u32[]{:S(2)}) copy-start(f32[1024,768]{1,0:T(8,128)} %copy-done.1) | copy-start | bytes 9437188
  162.1 3.8 %copy-start.6 = (bf16[4,2,128,768]{3,2,1,0:T(8,128)(2,1)S(1)}, bf16[4,2,128,768]{3,2,1,0:T(8,128)(2,1)}, u32[]{:S(2)}) copy-start(bf16[4,2,128,768]{3,2,1,0:T(8,128)(2,1)} %get-tuple-element.55) | copy-start | bytes 4718596
  165.8 2.6 copy-start.4
  165.8 2.6 copy-start.18
  302.5 3.8 %copy-start.8 = (bf16[4,2,128,768]{3,2,1,0:T(8,128)(2,1)S(1)}, bf16[4,2,128,768]{3,2,1,0:T(8,128)(2,1)}, u32[]{:S(2)}) copy-start(bf16[4,2,128,768]{3,2,1,0:T(8,128)(2,1)} %get-tuple-element.82) | copy-start | bytes 4718596
  306.2 5.5 %copy-start.11 = (bf16[4,1,128,768]{3,2,1,0:T(8,128)(2,1)S(1)}, bf16[4,1,128,768]{3,2,1,0:T(8,128)(2,1)}, u32[]{:S(2)}) copy-start(bf16[4,1,128,768]{3,2,1,0:T(8,128)(2,1)} %get-tuple-element.83) | copy-start | bytes 2359300
  306.2 5.5 %copy-start.12 = (bf16[4,1,128,768]{3,2,1,0:T(8,128)(2,1)S(1)}, bf16[4,1,128,768]{3,2,1,0:T(8,128)(2,1)}, u32[]{:S(2)}) copy-start(bf16[4,1,128,768]{3,2,1,0:T(8,128)(2,1)} %get-tuple-element.89) | copy-start | bytes 2359300
  310.3 1.9 copy-start.3
  312.2 2.2 copy-start.10
  314.4 1.7 copy-start.9
where the time goes:
time: 321 us; the launch traced here: 318 us
  Pallas kernels  244 us (76%)
  matrix products  29 us (9%)
  other arithmetic  19.4 us (6%)
  waiting for transfers between devices  10.9 us (3%)
  local copies, waits for them, and re-layouts  7.76 us (2%)
  starting transfers between devices  4.56 us (1%)
    pallas_call x1, Pallas kernels, attention_backward(): pl.pallas_call(functools.partial(attn_bwd_kernel, calls, dp_bits), grid=(...  65 us
    pallas_call x2, Pallas kernels, ffn(): pl.pallas_call(functools.partial(ffn_kernel, first, bits), grid_spec=pltp...  63.1 us
    pallas_call x1, Pallas kernels, finish(): pl.pallas_call(functools.partial(finish_kernel, calls, dp_bits), in_specs...  59.8 us
    pallas_call x1, Pallas kernels, enter(): pl.pallas_call(enter_kernel, in_specs=[pl.BlockSpec(memory_space=pl.ANY)]...  29.9 us
    pallas_call x1, Pallas kernels, attention_forward(): pl.pallas_call(attn_fwd_kernel, grid=(rows, pairs), in_specs=[pl.BlockSpe...  26.5 us
    dot_general x4, matrix products, mm(): return jnp.dot(a, b, preferred_element_type=F32)  13.6 us
    dot_general x3, matrix products, mm_tn(): return lax.dot_general(a, b, TN, preferred_element_type=F32)  12.8 us
  transfers between devices with their start and end apart: 8, of which 4 were waited for; matrix products, arithmetic and copies ran while one was open for 9% of the time, Pallas kernels for 10%

commit v1 on v0

--- a/solution.py
+++ b/solution.py
@@ -45,22 +45,37 @@
 
 
 def ffn_kernel(first, bits, info_ref, xm_ref, xo_ref, gm_ref, go_ref, u_ref, d_ref, *refs):
-    if first:
-        prev = (None,) * 4
-        outs, grads = refs[:4], refs[4:8]
-    else:
-        prev, outs, grads = refs[:4], refs[4:8], refs[8:12]
-    du_ref, dd_ref, act_ref, dh_ref = refs[-4:]
+    refs = list(refs)
+    prev = [] if first else draw(refs, 4)
+    outs, grads = draw(refs, 4), draw(refs, 4)
+    du_ref, dd_ref, act_ref, dh_ref, x_ref, g_ref = draw(refs, 6)
+    held, up_ref, keep_ref, send_ref, sem = draw(refs, 2), *refs
     e = pl.program_id(0)
     slots, model = xm_ref.shape
     cols = u_ref.shape[-1]
     tile = 256
     down = d_ref[0]
+    made = [0]
+
+    def local(src, dst):
+        made[0] += 1
+        return pltpu.make_async_copy(src, dst, sem.at[made[0] - 1])
+
+    loads = [
+        [local(x, x_ref.at[i]), local(g, g_ref.at[i])]
+        + [local(p, h.at[i]) for p, h in zip(prev[i::2], held)]
+        for i, (x, g) in enumerate(((xm_ref, gm_ref), (xo_ref, go_ref)))
+    ]
+    stores = [[local(h.at[i], out) for h, out in zip(held, outs[i::2])] for i in range(2)]
 
     @pl.when(e == 0)
     def _():
-        for out in outs:
-            out[slots - BLK :, :] = jnp.zeros((BLK, model), BF)
+        for copy in loads[0] + loads[1]:
+            copy.start()
+        if first:
+            for h in held:
+                for which in range(2):
+                    h[which, slots - BLK :, :] = jnp.zeros((BLK, model), BF)
 
     du_ref[...] = jnp.zeros_like(du_ref)
     dd_ref[...] = jnp.zeros_like(dd_ref)
@@ -68,8 +83,8 @@
     def chunk(which, block, count):
         size = count * BLK
         rows = pl.ds(pl.multiple_of(block * BLK, BLK), size)
-        x = (xm_ref, xo_ref)[which][rows, :]
-        g = (gm_ref, go_ref)[which][rows, :]
+        x = x_ref[which, rows, :]
+        g = g_ref[which, rows, :]
         for n in range(cols // tile):
             part = slice(n * tile, (n + 1) * tile)
             h = mm(x, u_ref[0, :, part])
@@ -80,50 +95,58 @@
             dh_ref[:size, part] = (da * (cdf + h * pdf)).astype(BF)
         act = act_ref[:size, :]
         dh = dh_ref[:size, :]
-        for slot, value in ((which, mm(act, down)), (2 + which, mm_nt(dh, u_ref[0]))):
-            if prev[slot] is not None:
-                value = value + prev[slot][rows, :].astype(F32)
-            outs[slot][rows, :] = value.astype(BF)
+        for slot, value in enumerate((mm(act, down), mm_nt(dh, u_ref[0]))):
+            if not first:
+                value = value + held[slot][which, rows, :].astype(F32)
+            held[slot][which, rows, :] = value.astype(BF)
         du_ref[...] += mm_tn(x, dh)
         dd_ref[...] += mm_tn(act, g)
 
-    for which in range(2):
+    def side(which, carry):
+        for i in range(2):
+
+            @pl.when((e == 0) & (which == i))
+            def _(i=i):
+                for copy in loads[i]:
+                    copy.wait()
+
         n0 = info_ref[2 * which]
         n1 = info_ref[2 * which + 1]
         start = jnp.where(e == 0, 0, n0)
         count = jnp.where(e == 0, n0, n1)
-
-        def four(i, carry, which=which, start=start):
+        fours = count // 4 - jnp.where((count % 4 == 1) & (count > 4), 1, 0)
+
+        def four(i, carry):
             chunk(which, start + 4 * i, 4)
             return carry
 
-        lax.fori_loop(0, count // 4, four, 0)
-        at2 = start + (count // 4) * 4
-
-        @pl.when((count // 2) % 2 == 1)
-        def _(which=which, at2=at2):
-            chunk(which, at2, 2)
-
-        at1 = start + (count // 2) * 2
-
-        @pl.when(count % 2 == 1)
-        def _(which=which, at1=at1):
-            chunk(which, at1, 1)
+        lax.fori_loop(0, fours, four, 0)
+        for left in (1, 2, 3, 5):
+
+            @pl.when(count - 4 * fours == left)
+            def _(left=left):
+                chunk(which, start + 4 * fours, left)
+
+        for i in range(2):
+
+            @pl.when((e == EXPERTS - 1) & (which == i))
+            def _(i=i):
+                for copy in stores[i]:
+                    copy.start()
+
+        return carry
+
+    lax.fori_loop(0, 2, side, 0)
 
     up_keep, up_send, down_keep, down_send = grads
     groups = 1 << bits
     per = model // groups
-    wide = down_keep.shape[2]
+    wide = keep_ref.shape[2]
     xbit, ybit = info_ref[4], info_ref[5]
-    for ref, here in ((up_keep, e == xbit), (up_send, e != xbit)):
-
-        @pl.when(here)
-        def _(ref=ref):
-            for p in range(groups):
-                ref[spot(p, range(bits))] = du_ref[p * per : (p + 1) * per, :].astype(BF)
-
+    for p in range(groups):
+        up_ref[e, spot(p, range(bits))] = du_ref[p * per : (p + 1) * per, :].astype(BF)
     for y in range(2):
-        for ref, here in ((down_keep, ybit == y), (down_send, ybit != y)):
+        for ref, here in ((keep_ref, ybit == y), (send_ref, ybit != y)):
 
             @pl.when(here)
             def _(ref=ref, y=y):
@@ -131,6 +154,38 @@
                     at = spot(p >> 1, range(bits - 3))
                     ref[at, e] = dd_ref[p * wide : (p + 1) * wide, :].astype(BF)
 
+    sends = []
+    for i in range(EXPERTS):
+        ups = local(up_ref.at[i], up_keep), local(up_ref.at[i], up_send)
+        downs = [
+            local(src.at[:, i], dst.at[:, i])
+            for src, dst in ((keep_ref, down_keep), (send_ref, down_send))
+        ]
+        sends.append((ups, downs))
+
+        @pl.when(e == i)
+        def _(ups=ups, downs=downs, i=i):
+            for copy in downs:
+                copy.start()
+            for copy, here in zip(ups, (xbit == i, xbit != i)):
+
+                @pl.when(here)
+                def _(copy=copy):
+                    copy.start()
+
+    @pl.when(e == EXPERTS - 1)
+    def _():
+        for copy in stores[0] + stores[1]:
+            copy.wait()
+        for i, (ups, downs) in enumerate(sends):
+            for copy in downs:
+                copy.wait()
+            for copy, here in zip(ups, (xbit == i, xbit != i)):
+
+                @pl.when(here)
+                def _(copy=copy):
+                    copy.wait()
+
 
 def spot(index, order):
     return functools.reduce(lambda acc, bit: 2 * acc + (index >> bit & 1), order, 0)
@@ -141,7 +196,7 @@
     hidden = up.shape[-1]
     cols = hidden // (2 * CALLS)
     bits = groups.bit_length() - 1
-    whole = pl.BlockSpec((slots, model), lambda e, i: (0, 0), pipeline_mode=pl.Buffered(1))
+    hbm = pl.BlockSpec(memory_space=pl.ANY)
     first = partial is None
     extra = () if first else tuple(partial)
     grads = [(groups, model // groups, model)] * 2
@@ -151,19 +206,26 @@
         grid_spec=pltpu.PrefetchScalarGridSpec(
             num_scalar_prefetch=1,
             grid=(EXPERTS,),
-            in_specs=[whole] * 4
+            in_specs=[hbm] * 4
             + [
                 pl.BlockSpec((1, model, cols), lambda e, i: (e, 0, i[6] * CALLS + call)),
                 pl.BlockSpec((1, cols, model), lambda e, i: (e, i[6] * CALLS + call, 0)),
             ]
-            + [whole] * len(extra),
-            out_specs=[pl.BlockSpec((slots, model), lambda e, i: (0, 0))] * 4
-            + [pl.BlockSpec(g, lambda e, i, n=len(g): (0,) * n) for g in grads],
+            + [hbm] * len(extra),
+            out_specs=[hbm] * 8,
             scratch_shapes=[
                 pltpu.VMEM((model, cols), F32),
                 pltpu.VMEM((cols, model), F32),
-                pltpu.VMEM((4 * BLK, cols), BF),
-                pltpu.VMEM((4 * BLK, cols), BF),
+                pltpu.VMEM((5 * BLK, cols), BF),
+                pltpu.VMEM((5 * BLK, cols), BF),
+                pltpu.VMEM((2, slots, model), BF),
+                pltpu.VMEM((2, slots, model), BF),
+                pltpu.VMEM((2, slots, model), BF),
+                pltpu.VMEM((2, slots, model), BF),
+                pltpu.VMEM((EXPERTS,) + grads[0], BF),
+                pltpu.VMEM(grads[2], BF),
+                pltpu.VMEM(grads[2], BF),
+                pltpu.SemaphoreType.DMA((24,)),
             ],
         ),
         out_shape=[jax.ShapeDtypeStruct((slots, model), BF)] * 4
@@ -326,7 +388,7 @@
     lane = lax.broadcasted_iota(jnp.int32, (1, width), 1) // HEAD_DIM
     zero = jnp.zeros((), BF)
     per = width // HEAD_DIM
-    step = 2 * length
+    step = seq
     ks = [jnp.where(lane == h, k, zero) for h in range(per)]
     for b in range(seq // step):
         cols = slice(b * step, (b + 1) * step)
@@ -339,7 +401,7 @@
             parts.append(mm(vt[h * HEAD_DIM : (h + 1) * HEAD_DIM], e.astype(BF)) * (1.0 / total))
             lse_ref[0, 0, h : h + 1, cols] = top + jnp.log(total)
         out = jnp.concatenate(parts, axis=0).T.astype(BF)
-        o_ref[2 * b : 2 * b + 2, 0] = out.reshape(2, length, width)
+        o_ref[:, 0] = out.reshape(sub, length, width)
 
 
 def attention_forward(segment, qkv, cotangent):
@@ -480,7 +542,7 @@
     lane = lax.broadcasted_iota(jnp.int32, (1, width), 1) // HEAD_DIM
     zero = jnp.zeros((), BF)
     per = width // HEAD_DIM
-    step = 2 * length
+    step = seq
     dk = jnp.zeros((seq, width), F32)
     dv = jnp.zeros((seq, width), F32)
     dqs = [[] for _ in range(seq // step)]

time: 321 us -> 311 us (0.969)
  Pallas kernels: 244 us -> 229 us
  starting transfers between devices: 4.56 us -> 9.11 us
    pallas_call x2, Pallas kernels: 63.1 us -> 50.3 us  [ffn(): pl.pallas_call(functools.partial(ffn_kernel, first, bits), grid_spec=pltp...]
    ppermute x2, starting transfers between devices: 1.95 us -> 6.5 us  [body(): came[1].append(dflip[0](down_send))]
  transfers between devices with their start and end apart: 8 -> 8, of which waited for: 4 -> 5; matrix products, arithmetic and copies ran while one was open for 9% -> 10% of each run, Pallas kernels for 10% -> 8%
where the time goes in v1:
time: 311 us; the launch traced here: 306 us
  Pallas kernels  229 us (74%)
  matrix products  29 us (9%)
  other arithmetic  19.4 us (6%)
  waiting for transfers between devices  10.6 us (3%)
  starting transfers between devices  9.11 us (3%)
  local copies, waits for them, and re-layouts  6.76 us (2%)
    pallas_call x1, Pallas kernels, attention_backward(): pl.pallas_call(functools.partial(attn_bwd_kernel, calls, dp_bits), grid=(...  65.2 us
    pallas_call x1, Pallas kernels, finish(): pl.pallas_call(functools.partial(finish_kernel, calls, dp_bits), in_specs...  59.9 us
    pallas_call x2, Pallas kernels, ffn(): pl.pallas_call(functools.partial(ffn_kernel, first, bits), grid_spec=pltp...  50.3 us
    pallas_call x1, Pallas kernels, enter(): pl.pallas_call(enter_kernel, in_specs=[pl.BlockSpec(memory_space=pl.ANY)]...  29.9 us
    pallas_call x1, Pallas kernels, attention_forward(): pl.pallas_call(attn_fwd_kernel, grid=(rows, pairs), in_specs=[pl.BlockSpe...  23.7 us
    dot_general x4, matrix products, mm(): return jnp.dot(a, b, preferred_element_type=F32)  13.6 us
    dot_general x3, matrix products, mm_tn(): return lax.dot_general(a, b, TN, preferred_element_type=F32)  12.8 us
    ppermute x2, starting transfers between devices, body(): came[1].append(dflip[0](down_send))  6.5 us
  transfers between devices with their start and end apart: 8, of which 5 were waited for; matrix products, arithmetic and copies ran while one was open for 10% of the time, Pallas kernels for 8%

profile of v1, /device:TPU:0, one launch (start us, length us, event | category | flops | bytes accessed | tf_op | source)
XLA Modules:
  0.0 306.0 jit_solution(16356024886885302361)
XLA Ops:
  0.7 0.8 fusion.48
  1.5 0.7 constant_dynamic-slice_fusion.3
  2.2 29.9 %enter.1 = (bf16[4,2,128,768]{3,2,1,0:T(8,128)(2,1)}, s32[4,2,2,128]{3,2,1,0:T(2,128)}, f32[4,2,128,1]{3,2,1,0:T(8,128)}, bf16[4,2,128,768]{3,2,1,0:T(8,128)(2,1)}, bf16[4,2,128,2304]{3,2,1,0:T(8,128)(2,1)}) custom-call(f32[4,2,128,768]{3,2,1,0:T(8,128)} %bitcast.64, s32[2,2,2,128]{3,2,1,0:T(2,128)} %bitcast.71, f32[2,768]{1,0:T(2,128)} %refs_12_.1, ...), custom_call_target="tpu_custom_call" | custom-call | flops 3623878656 | bytes 41943040 | tf_op jit(solution)/shard_map/enter/pallas_call | solution.py:993
  32.2 0.7 dynamic-slice_compare_fusion
  32.9 0.2 fusion.26
  33.2 0.5 slice.43
  34.4 0.2 subtract_reduce_fusion
  34.6 0.6 broadcast_in_dim.74.segr_ref.refs_1_
  35.2 1.0 copy.23.segc_ref.refs_0_
  36.3 23.7 %attn_fwd.1 = (bf16[4,2,128,768]{3,2,1,0:T(8,128)(2,1)}, f32[2,6,2,512]{3,2,1,0:T(2,128)}, bf16[4,2,128,768]{3,2,1,0:T(8,128)(2,1)}) custom-call(s32[2,512,1]{2,1,0:T(8,128)} %copy.23.segc_ref.refs_0_, s32[2,1,512]{2,1,0:T(1,128)} %broadcast_in_dim.74.segr_ref.refs_1_, bf16[4,2,128,2304]{3,2,1,0:T(8,128)(2,1)} %get-tuple-element.52.q_ref.k_ref.v_ref.refs_2_.refs_3_.refs_4_, ...), custom_call_target="tpu_custom_call" | custom-call | flops 3221225472 | bytes 6291456 | tf_op jit(solution)/shard_map/attn_fwd/pallas_call | solution.py:414
  59.9 4.9 %fusion.5.gm_ref = bf16[1152,768]{1,0:T(8,128)(2,1)} fusion(bf16[1024,768]{1,0:T(8,128)(2,1)} %bitcast.68, s32[1024]{0:T(1024)S(1)} %fusion.32), kind=kOutput, calls=%fused_computation.8 | convolution fusion | flops 1814003712 | bytes 3346432 | tf_op jit(solution)/shard_map/dot_general | solution.py:24
  64.9 0.2 compare_reduce_fusion
  65.1 4.5 %fusion.38 = (f32[1024]{0:T(1024)S(1)}, f32[1024,768]{1,0:T(8,128)S(1)}, f32[1024,768]{1,0:T(8,128)}) fusion(bf16[4,2,128,768]{3,2,1,0:T(8,128)(2,1)S(1)} %copy-done.5, bf16[1024,768]{1,0:T(8,128)(2,1)} %bitcast.66, bf16[768,768]{1,0:T(8,128)(2,1)S(1)} %copy-done), kind=kOutput, calls=%fused_computation.89 | convolution fusion | flops 1210317824 | bytes 10620928 | tf_op jit(solution)/shard_map/dot_general | solution.py:24
  69.6 0.5 multiply_reduce_fusion.1
  70.2 0.2 copy-done.15
  70.4 4.0 %fusion.4.xm_ref = bf16[1152,768]{1,0:T(8,128)(2,1)} fusion(s32[1024]{0:T(1024)S(1)} %fusion.32, f32[1024,768]{1,0:T(8,128)S(1)} %get-tuple-element.113, f32[768]{0:T(1024)S(1)} %get-tuple-element.107, f32[768]{0:T(1024)S(1)} %get-tuple-element.106, f32[768]{0:T(1024)S(1)} %get-tuple-element.122, f32[768]{0:T(1024)S(1)} %get-tuple-element.123, ...), kind=kOutput, calls=%fused_computation.7 | convolution fusion | flops 1819508736 | bytes 4940800 | tf_op jit(solution)/shard_map/dot_general | solution.py:24
  74.4 0.5 collective-permute-start
  75.1 0.2 fusion.35
  75.3 0.6 concatenate.6.info_ref
  75.9 2.7 collective-permute-done.xo_ref
  78.6 24.8 %ffn.2 = (bf16[1152,768]{1,0:T(8,128)(2,1)}, bf16[1152,768]{1,0:T(8,128)(2,1)}, bf16[1152,768]{1,0:T(8,128)(2,1)}, bf16[1152,768]{1,0:T(8,128)(2,1)}, bf16[8,96,...) custom-call(s32[7]{0:T(128)} %concatenate.6.info_ref, ...), custom_call_target="tpu_custom_call" | custom-call | flops 16307453952 | bytes 41943040 | tf_op jit(solution)/shard_map/ffn/pallas_call | solution.py:204
  103.4 1.2 collective-permute-start.2
  104.6 4.0 %collective-permute-start.3 = (bf16[1,2,384,768]{3,2,1,0:T(8,128)(2,1)}, bf16[1,2,384,768]{3,2,1,0:T(8,128)(2,1)}, u32[]{:S(2)}, u32[]{:S(2)}) collective-permute-start(bf16[1,2,384,768]{3,2,1,0:T(8,128)(2,1)} %get-tuple-element.67), channel_id=1, source_target_pairs={{0,4},{4,0},{8,12},{12,8},{16,20},{20,16},{24,28},{28,24},{1,5},{5... | collective-permute-start | bytes 3538952 | tf_op jit(solution)/shard_map/ppermute | solution.py:1125
  108.6 25.5 %ffn.3 = (bf16[1152,768]{1,0:T(8,128)(2,1)}, bf16[1152,768]{1,0:T(8,128)(2,1)}, bf16[1152,768]{1,0:T(8,128)(2,1)}, bf16[1152,768]{1,0:T(8,128)(2,1)}, bf16[8,96,...) custom-call(s32[7]{0:T(128)} %concatenate.6.info_ref, ...), custom_call_target="tpu_custom_call" | custom-call | flops 16307453952 | bytes 41943040 | tf_op jit(solution)/shard_map/ffn/pallas_call | solution.py:204
  134.1 1.0 collective-permute-done.3.refs_19_
  135.2 0.9 collective-permute-start.5
  136.1 2.5 collective-permute-start.6
  138.6 0.5 collective-permute-done.4
  139.1 6.6 %select_reduce_fusion.1 = (f32[768]{0:T(1024)S(1)}, f32[768]{0:T(1024)S(1)}, f32[1024]{0:T(1024)S(1)}, f32[1024]{0:T(1024)S(1)}, f32[768]{0:T(1024)S(1)}, /*index=5*/f32[768]{0:T(1024)S(1)}, f32[1024,768]{1,0:T(8,128)S(1)}) fusion(pred[1024]{0:T(1024)(128)(4,1)S(1)} %eq.63, f32[768]{0:T(1024)S(1)} %get-tuple-element.122, f32[768]{0:T(1024)S(1)} %get-tuple-element.123, ...), kind=kOutput, calls=%fused_computation.15 | convolution fusion | flops 1826581504 | bytes 9870336 | tf_op jit(solution)/shard_map/dot_general | solution.py:32
  145.7 3.0 add_convert_fusion.1
  148.7 2.6 convolution_convert_fusion
  151.3 0.6 pad_maximum_fusion.2.refs_5_
  151.9 0.6 pad_maximum_fusion.1.refs_4_
  152.5 2.6 convolution_convert_fusion.1
  155.1 3.7 %add_convert_fusion = bf16[1024,768]{1,0:T(8,128)(2,1)} fusion(f32[1024,768]{1,0:T(8,128)S(1)} %copy-done.4, bf16[1152,768]{1,0:T(8,128)(2,1)S(1)} %copy-done.18, bf16[1152,768]{1,0:T(8,128)(2,1)S(1)} %collective-permute-done.7, s32[1024]{0:T(1024)S(1)} %fusion.32), kind=kOutput, calls=%fused_computation.18 | convolution fusion | flops 1815576576 | bytes 8261632 | tf_op jit(solution)/shard_map/dot_general | solution.py:32
  158.8 5.1 %collective-permute-done.5 = bf16[8,96,768]{2,1,0:T(8,128)(2,1)} collective-permute-done((bf16[8,96,768]{2,1,0:T(8,128)(2,1)}, bf16[8,96,768]{2,1,0:T(8,128)(2,1)}, u32[]{:S(2)}, u32[]{:S(2)}) %collective-permute-start.5) | collective-permute-done | bytes 1179680 | tf_op jit(solution)/shard_map/ppermute | solution.py:1124
  163.9 1.3 collective-permute-done.6.refs_20_
  165.2 65.2 %attn_bwd.1 = (bf16[8,96,2304]{2,1,0:T(8,128)(2,1)}, f32[4,768]{1,0:T(4,128)}, bf16[4,1,128,768]{3,2,1,0:T(8,128)(2,1)}, bf16[2,2,96,768]{3,2,1,0:T(8,128)(2,1)}...) custom-call(s32[2,512,1]{2,1,0:T(8,128)} %copy.23.segc_ref.refs_0_, ...), custom_call_target="tpu_custom_call" | custom-call | flops 15300820992 | bytes 104857600 | tf_op jit(solution)/shard_map/attn_bwd/pallas_call | solution.py:668
  230.4 59.9 %finish.1 = (bf16[96,3072]{1,0:T(8,128)(2,1)}, bf16[2,96,3072]{2,1,0:T(8,128)(2,1)}, bf16[2,384,768]{2,1,0:T(8,128)(2,1)}, f32[8,768]{1,0:T(8,128)}, bf16[4,1,128,768]{3,2,1,0:T(8,128)(2,1)}) custom-call(bf16[2,2,96,768]{3,2,1,0:T(8,128)(2,1)} %get-tuple-element.84.refs_0_, bf16[8,96,2304]{2,1,0:T(8,128)(2,1)} %get-tuple-element.85.refs_1_, ...), custom_call_target="tpu_custom_call" | custom-call | bytes 104857600 | tf_op jit(solution)/shard_map/finish/pallas_call | solution.py:900
  290.4 1.8 slice_convert_fusion.1
  292.1 2.0 slice_convert_fusion
  294.1 4.0 %convert_add_fusion.1 = f32[8,128,768]{2,1,0:T(8,128)} fusion(f32[8,128,768]{2,1,0:T(8,128)} %param.12, bf16[4,2,128,768]{3,2,1,0:T(8,128)(2,1)S(1)} %copy-done.8), kind=kLoop, calls=%fused_computation.12 | loop fusion | flops 1572864 | bytes 7864320 | tf_op jit(solution)/shard_map/add | solution.py:1147
  298.1 0.9 constant_dynamic-slice_fusion
  299.1 0.6 fusion.39
  299.8 0.3 copy-done.3
  300.0 2.2 convert_add_fusion
  302.3 1.7 convert_element_type.86
  303.9 1.6 convert_element_type.87
  (62 shorter events, 0.8 us)
Async XLA Ops:
  0.6 64.5 %copy-start = (bf16[768,768]{1,0:T(8,128)(2,1)S(1)}, bf16[768,768]{1,0:T(8,128)(2,1)}, u32[]{:S(2)}) copy-start(bf16[768,768]{1,0:T(8,128)(2,1)} %param.18) | copy-start | bytes 3538948
  59.9 5.0 %copy-start.13 = (f32[4,2,128,1]{3,2,1,0:T(8,128)S(1)}, f32[4,2,128,1]{3,2,1,0:T(8,128)}, u32[]{:S(2)}) copy-start(f32[4,2,128,1]{3,2,1,0:T(8,128)} %get-tuple-element.57.refs_11_) | copy-start | bytes 12292
  59.9 5.2 %copy-start.5 = (bf16[4,2,128,768]{3,2,1,0:T(8,128)(2,1)S(1)}, bf16[4,2,128,768]{3,2,1,0:T(8,128)(2,1)}, u32[]{:S(2)}) copy-start(bf16[4,2,128,768]{3,2,1,0:T(8,128)(2,1)} %get-tuple-element.54.refs_9_) | copy-start | bytes 4718596
  64.9 11.1 %collective-permute-start.1 = (bf16[1152,768]{1,0:T(8,128)(2,1)}, bf16[1152,768]{1,0:T(8,128)(2,1)}, u32[]{:S(2)}, u32[]{:S(2)}) collective-permute-start(bf16[1152,768]{1,0:T(8,128)(2,1)} %fusion.5.gm_ref), channel_id=1, source_target_pairs={{0,1},{1,0},{2,3},{3,2},{4,5},{5,4},{6,7},{7,6},{8,9},{9,8},{10,11... | collective-permute-start | bytes 5308424 | tf_op jit(solution)/shard_map/ppermute | solution.py:1107
  69.6 4.8 %copy-start.1 = (f32[1024,768]{1,0:T(8,128)}, f32[1024,768]{1,0:T(8,128)S(1)}, u32[]{:S(2)}) copy-start(f32[1024,768]{1,0:T(8,128)S(1)} %get-tuple-element.113) | copy-start | bytes 9437188
  69.6 0.7 copy-start.15
  69.6 0.8 copy-start.16
  70.4 4.5 %copy-start.14 = (s32[4,2,2,128]{3,2,1,0:T(2,128)S(1)}, s32[4,2,2,128]{3,2,1,0:T(2,128)}, u32[]{:S(2)}) copy-start(s32[4,2,2,128]{3,2,1,0:T(2,128)} %get-tuple-element.56) | copy-start | bytes 24580
  74.4 4.2 %collective-permute-start = (bf16[1152,768]{1,0:T(8,128)(2,1)}, bf16[1152,768]{1,0:T(8,128)(2,1)}, u32[]{:S(2)}, u32[]{:S(2)}) collective-permute-start(bf16[1152,768]{1,0:T(8,128)(2,1)} %fusion.4.xm_ref), channel_id=1, source_target_pairs={{0,1},{1,0},{2,3},{3,2},{4,5},{5,4},{6,7},{7,6},{8,9},{9,8},{10,11... | collective-permute-start | bytes 5308424 | tf_op jit(solution)/shard_map/ppermute | solution.py:1115
  103.4 30.7 %collective-permute-start.2 = (bf16[8,96,768]{2,1,0:T(8,128)(2,1)}, bf16[8,96,768]{2,1,0:T(8,128)(2,1)S(1)}, u32[]{:S(2)}, u32[]{:S(2)}) collective-permute-start(bf16[8,96,768]{2,1,0:T(8,128)(2,1)} %get-tuple-element.66), channel_id=1, source_target_pairs={{0,2},{1,3},{2,0},{3,1},{4,6},{5,7},{6,4},{7,5},{8,10},{9,11},{10,... | collective-permute-start | bytes 3538952 | tf_op jit(solution)/shard_map/ppermute | solution.py:1124
  104.6 30.5 %collective-permute-start.3 = (bf16[1,2,384,768]{3,2,1,0:T(8,128)(2,1)}, bf16[1,2,384,768]{3,2,1,0:T(8,128)(2,1)}, u32[]{:S(2)}, u32[]{:S(2)}) collective-permute-start(bf16[1,2,384,768]{3,2,1,0:T(8,128)(2,1)} %get-tuple-element.67), channel_id=1, source_target_pairs={{0,4},{4,0},{8,12},{12,8},{16,20},{20,16},{24,28},{28,24},{1,5},{5... | collective-permute-start | bytes 3538952 | tf_op jit(solution)/shard_map/ppermute | solution.py:1125
  134.1 1.1 copy-start.17
  135.2 3.9 %collective-permute-start.4 = (bf16[1152,768]{1,0:T(8,128)(2,1)}, bf16[1152,768]{1,0:T(8,128)(2,1)S(1)}, u32[]{:S(2)}, u32[]{:S(2)}) collective-permute-start(bf16[1152,768]{1,0:T(8,128)(2,1)} %get-tuple-element.69), channel_id=1, source_target_pairs={{0,1},{1,0},{2,3},{3,2},{4,5},{5,4},{6,7},{7,6},{8,9},{9,8},{10,11... | collective-permute-start | bytes 5308424 | tf_op jit(solution)/shard_map/ppermute | solution.py:1130
  135.2 28.7 %collective-permute-start.5 = (bf16[8,96,768]{2,1,0:T(8,128)(2,1)}, bf16[8,96,768]{2,1,0:T(8,128)(2,1)}, u32[]{:S(2)}, u32[]{:S(2)}) collective-permute-start(bf16[8,96,768]{2,1,0:T(8,128)(2,1)} %get-tuple-element.75), channel_id=1, source_target_pairs={{0,2},{1,3},{2,0},{3,1},{4,6},{5,7},{6,4},{7,5},{8,10},{9,11},{10,... | collective-permute-start | bytes 3538952 | tf_op jit(solution)/shard_map/ppermute | solution.py:1124
  136.1 9.6 %copy-start.7 = (bf16[4,2,128,768]{3,2,1,0:T(8,128)(2,1)S(1)}, bf16[4,2,128,768]{3,2,1,0:T(8,128)(2,1)}, u32[]{:S(2)}) copy-start(bf16[4,2,128,768]{3,2,1,0:T(8,128)(2,1)} %get-tuple-element.53) | copy-start | bytes 4718596
  136.1 29.1 %collective-permute-start.6 = (bf16[1,2,384,768]{3,2,1,0:T(8,128)(2,1)}, bf16[1,2,384,768]{3,2,1,0:T(8,128)(2,1)}, u32[]{:S(2)}, u32[]{:S(2)}) collective-permute-start(bf16[1,2,384,768]{3,2,1,0:T(8,128)(2,1)} %get-tuple-element.79), channel_id=1, source_target_pairs={{0,4},{4,0},{8,12},{12,8},{16,20},{20,16},{24,28},{28,24},{1,5},{5... | collective-permute-start | bytes 3538952 | tf_op jit(solution)/shard_map/ppermute | solution.py:1125
  138.6 16.4 %collective-permute-start.7 = (bf16[1152,768]{1,0:T(8,128)(2,1)}, bf16[1152,768]{1,0:T(8,128)(2,1)S(1)}, u32[]{:S(2)}, u32[]{:S(2)}) collective-permute-start(bf16[1152,768]{1,0:T(8,128)(2,1)} %get-tuple-element.81), channel_id=1, source_target_pairs={{0,1},{1,0},{2,3},{3,2},{4,5},{5,4},{6,7},{7,6},{8,9},{9,8},{10,11... | collective-permute-start | bytes 5308424 | tf_op jit(solution)/shard_map/ppermute | solution.py:1132
  139.1 6.6 %copy-start.2 = (f32[1024,768]{1,0:T(8,128)S(1)}, f32[1024,768]{1,0:T(8,128)}, u32[]{:S(2)}) copy-start(f32[1024,768]{1,0:T(8,128)} %copy-done.1) | copy-start | bytes 9437188
  148.7 3.8 %copy-start.6 = (bf16[4,2,128,768]{3,2,1,0:T(8,128)(2,1)S(1)}, bf16[4,2,128,768]{3,2,1,0:T(8,128)(2,1)}, u32[]{:S(2)}) copy-start(bf16[4,2,128,768]{3,2,1,0:T(8,128)(2,1)} %get-tuple-element.55) | copy-start | bytes 4718596
  152.5 2.6 copy-start.4
  152.5 2.6 copy-start.18
  290.4 3.8 %copy-start.8 = (bf16[4,2,128,768]{3,2,1,0:T(8,128)(2,1)S(1)}, bf16[4,2,128,768]{3,2,1,0:T(8,128)(2,1)}, u32[]{:S(2)}) copy-start(bf16[4,2,128,768]{3,2,1,0:T(8,128)(2,1)} %get-tuple-element.82) | copy-start | bytes 4718596
  294.1 5.5 %copy-start.11 = (bf16[4,1,128,768]{3,2,1,0:T(8,128)(2,1)S(1)}, bf16[4,1,128,768]{3,2,1,0:T(8,128)(2,1)}, u32[]{:S(2)}) copy-start(bf16[4,1,128,768]{3,2,1,0:T(8,128)(2,1)} %get-tuple-element.83) | copy-start | bytes 2359300
  294.1 5.5 %copy-start.12 = (bf16[4,1,128,768]{3,2,1,0:T(8,128)(2,1)S(1)}, bf16[4,1,128,768]{3,2,1,0:T(8,128)(2,1)}, u32[]{:S(2)}) copy-start(bf16[4,1,128,768]{3,2,1,0:T(8,128)(2,1)} %get-tuple-element.89) | copy-start | bytes 2359300
  298.1 1.9 copy-start.3
  300.0 2.2 copy-start.10
  302.3 1.7 copy-start.9
